TPU v7x, 32 devices: a whole 2x2x4 slice. The times are simulated.
32 devices in a mesh: grp: 4 (over z), seq: 8 (over y, x, core).
Axes of the slice: x: 2, y: 2, z: 4, core: 2. Of those that a mesh axis runs over, the one named last changes fastest.
Arguments:
- tokens: bfloat16 [4096, 2048], P(('grp', 'seq')), may hold values from -6 to 6
- norm_gains: float32 [2, 2048], replicated, may hold values from 0.5 to 1.5
- norm_biases: float32 [2, 2048], replicated, may hold values from -1 to 1
- mix_weight: bfloat16 [2048, 3, 2048], P(None, None, 'seq'), may hold values from -0.125 to 0.125
- mix_bias: bfloat16 [3, 2048], P(None, 'seq'), may hold values from -1.796875 to 1.796875
- out_weight: bfloat16 [2048, 2048], P('seq'), may hold values from -0.5 to 0.5
- gate_up_weight: bfloat16 [2048, 2, 5632], P(None, None, 'seq'), may hold values from -0.125 to 0.125
- down_weight: bfloat16 [5632, 2048], P('seq'), may hold values from -0.078125 to 0.078125
- row_lengths: int32 [8], replicated, may hold values from 128 to 1024, as said below
- row_group: int32 [8], replicated, may hold values from 0 to 3, as said below
- cotangent: bfloat16 [4096, 2048], P(('grp', 'seq')), may hold values from -6 to 6
Outputs:
- layer_out: bfloat16 [4096, 2048], P(('grp', 'seq'))
- tokens_grad: bfloat16 [4096, 2048], P(('grp', 'seq'))
- gains_grad: float32 [2, 2048], replicated
- biases_grad: float32 [2, 2048], replicated
- mix_grad: float32 [2048, 3, 2048], P(None, None, 'seq')
- mix_bias_grad: float32 [3, 2048], P(None, 'seq')
- out_grad: float32 [2048, 2048], P('seq')
- gate_up_grad: float32 [2048, 2, 5632], P(None, None, 'seq')
- down_grad: float32 [5632, 2048], P('seq')
Inputs may be any that keep to these rules, and one draw needn't show every extreme that they name: `row_lengths`: rows 0 to 1 are 1024 long; every other row's length is a multiple of 128 and at most 256. `row_group`: each of rows 0 to 1 fills a group alone; every other group holds exactly three of the other rows.
All inputs are finite; a program needn't handle non-finite values.
Results may differ from a plain program's by a relative error of at most 0.02.
Values may be sent and summed in bfloat16 or wider, within the bound.
A program may use at most 320 MiB of HBM per device.

v0:
```python
import functools
import math

import jax
import jax.numpy as jnp
from jax import lax
from jax.experimental import pallas as pl
from jax.experimental.pallas import tpu as pltpu
from jax.sharding import PartitionSpec as P

HEAD_DIM = 64
ROT = 16


EPS = 1e-05
NEG = -1e30
BASE = 10000.0


def layer_norm(values, gain, bias):
    centered = values - jnp.mean(values, axis=-1, keepdims=True)
    scale = lax.rsqrt(jnp.mean(centered * centered, axis=-1, keepdims=True) + EPS)
    unit = centered * scale
    return (unit * gain + bias, unit, scale)


def norm_back(incoming, unit, scale, gain):
    along = incoming * gain
    inner = jnp.mean(along, axis=-1, keepdims=True)
    cross = jnp.mean(along * unit, axis=-1, keepdims=True)
    return (
        scale * (along - inner - unit * cross),
        jnp.sum(incoming * unit, axis=0),
        jnp.sum(incoming, axis=0),
    )


def rotate(values, where, sign):
    half = ROT // 2
    freq = BASE ** (-jnp.arange(half, dtype=jnp.float32) / half)
    angle = where.astype(jnp.float32)[:, None] * freq[None, :]
    cosine = jnp.cos(angle)[:, None, :]
    sine = sign * jnp.sin(angle)[:, None, :]
    first = values[..., :half]
    second = values[..., half:ROT]
    return jnp.concatenate(
        [first * cosine - second * sine, second * cosine + first * sine, values[..., ROT:]], axis=-1
    )


def unrotate(lowered, where):
    wide = lowered.astype(jnp.float32)
    turned = jnp.stack(
        [rotate(wide[:, 0], where, -1.0), rotate(wide[:, 1], where, -1.0), wide[:, 2]], axis=1
    )
    return turned.reshape(lowered.shape[0], 3, -1).astype(jnp.bfloat16)


def slot_rows(row_lengths, row_group, group, slots):
    order = jnp.arange(row_lengths.shape[0], dtype=jnp.int32)
    same = row_group == group
    earlier = (order[:, None] > order[None, :]) & same[None, :]
    begin = jnp.sum(jnp.where(earlier, row_lengths[None, :], 0), axis=1)
    finish = begin + row_lengths
    inside = same[None, :] & (slots[:, None] >= begin[None, :]) & (slots[:, None] < finish[None, :])
    label = jnp.sum(jnp.where(inside, order[None, :] + 1, 0), axis=1) - 1
    offset = jnp.sum(jnp.where(inside, slots[:, None] - begin[None, :], 0), axis=1)
    load = jnp.sum(jnp.where(same, row_lengths, 0))
    return (label, jnp.where(label < 0, slots - load, offset))


def block_scores(query, key, label, start, block):
    part = lax.dynamic_slice_in_dim(query, start, block, 0)
    rows = start + jnp.arange(block, dtype=jnp.int32)
    columns = jnp.arange(label.shape[0], dtype=jnp.int32)
    label_rows = lax.dynamic_slice_in_dim(label, start, block, 0)
    allowed = (label_rows[:, None] == label[None, :]) & (rows[:, None] >= columns[None, :])
    scores = jnp.einsum("qhe,khe->hqk", part, key, preferred_element_type=jnp.float32) * (
        1.0 / math.sqrt(query.shape[-1])
    )
    return (part, jnp.where(allowed[None], scores, NEG))


def attend(query, key, value, label, block):

    def one_block(index):
        part, scores = block_scores(query, key, label, index * block, block)
        top = jnp.max(scores, axis=-1, keepdims=True)
        weights = jnp.exp(scores - top)
        totals = jnp.sum(weights, axis=-1, keepdims=True)
        probs = (weights / totals).astype(jnp.bfloat16)
        mixed = jnp.einsum("hqk,khe->qhe", probs, value, preferred_element_type=jnp.float32)
        return (mixed, top[..., 0] + jnp.log(totals[..., 0]))

    mixed, log_totals = lax.map(one_block, jnp.arange(query.shape[0] // block, dtype=jnp.int32))
    return (mixed.reshape(query.shape), log_totals)


def attend_back(query, key, value, label, log_totals, mixed_back, block):
    scale = 1.0 / math.sqrt(query.shape[-1])

    def one_block(carry, index):
        key_back, value_back = carry
        start = index * block
        part, scores = block_scores(query, key, label, start, block)
        back_part = lax.dynamic_slice_in_dim(mixed_back, start, block, 0)
        probs = jnp.exp(scores - log_totals[index][..., None])
        value_back = value_back + jnp.einsum(
            "hqk,qhe->khe",
            probs.astype(jnp.bfloat16),
            back_part,
            preferred_element_type=jnp.float32,
        )
        probs_back = jnp.einsum(
            "qhe,khe->hqk", back_part, value, preferred_element_type=jnp.float32
        )
        inner = jnp.sum(probs_back * probs, axis=-1, keepdims=True)
        score_back = (probs * (probs_back - inner)).astype(jnp.bfloat16)
        query_back = (
            jnp.einsum("hqk,khe->qhe", score_back, key, preferred_element_type=jnp.float32) * scale
        )
        key_back = (
            key_back
            + jnp.einsum("hqk,qhe->khe", score_back, part, preferred_element_type=jnp.float32)
            * scale
        )
        return ((key_back, value_back), query_back)

    empty = jnp.zeros(key.shape, jnp.float32)
    (key_back, value_back), query_back = lax.scan(
        one_block, (empty, empty), jnp.arange(query.shape[0] // block, dtype=jnp.int32)
    )
    return (query_back.reshape(query.shape), key_back, value_back)


def silu_parts(gate_up):
    gate = gate_up[:, 0]
    upper = gate_up[:, 1]
    sigma = jax.nn.sigmoid(gate)
    return (gate * sigma * upper, gate, upper, sigma)


def gate_back(hidden_back, gate, upper, sigma):
    gate_part = hidden_back * upper * sigma * (1.0 + gate * (1.0 - sigma))
    up_part = hidden_back * gate * sigma
    return jnp.stack([gate_part, up_part], axis=1).astype(jnp.bfloat16)


def gather_rows(values):
    return lax.all_gather(values, "seq", axis=0, tiled=True)


def summed_rows(product, left):
    return lax.psum_scatter(
        product(left).astype(jnp.bfloat16), "seq", scatter_dimension=0, tiled=True
    ).astype(jnp.float32)


def plain_device(
    tokens,
    norm_gains,
    norm_biases,
    mix_weight,
    mix_bias,
    out_weight,
    gate_up_weight,
    down_weight,
    row_lengths,
    row_group,
    cotangent,
):
    seq_count = lax.axis_size("seq")
    shard = lax.axis_index("seq")
    group = lax.axis_index("grp")
    slots_dev = tokens.shape[0]
    width = tokens.shape[1]
    group_slots = slots_dev * seq_count
    block = min(512, group_slots)
    local_width = width // seq_count
    local_heads = local_width // HEAD_DIM
    mine = shard * slots_dev + jnp.arange(slots_dev, dtype=jnp.int32)
    label_mine, place_mine = slot_rows(row_lengths, row_group, group, mine)
    label_all, place_all = slot_rows(
        row_lengths, row_group, group, jnp.arange(group_slots, dtype=jnp.int32)
    )
    inputs = tokens.astype(jnp.float32)
    upstream = cotangent.astype(jnp.float32) * (label_mine >= 0).astype(jnp.float32)[:, None]
    upstream_low = upstream.astype(jnp.bfloat16)
    normed, unit_one, scale_one = layer_norm(inputs, norm_gains[0], norm_biases[0])
    normed_all = gather_rows(normed.astype(jnp.bfloat16))
    up_four = lax.all_gather(upstream_low, ("grp", "seq"), axis=0, tiled=True)
    upstream_all = lax.dynamic_slice_in_dim(up_four, group * group_slots, group_slots, 0)
    mixin = jnp.einsum(
        "td,dcf->tcf", normed_all, mix_weight, preferred_element_type=jnp.float32
    ) + mix_bias.astype(jnp.float32)
    heads_in = mixin.reshape(group_slots, 3, local_heads, HEAD_DIM)
    query = rotate(heads_in[:, 0], place_all, 1.0).astype(jnp.bfloat16)
    key = rotate(heads_in[:, 1], place_all, 1.0).astype(jnp.bfloat16)
    value = heads_in[:, 2].astype(jnp.bfloat16)
    mixed, log_totals = attend(query, key, value, label_all, block)
    attended = mixed.reshape(group_slots, local_width).astype(jnp.bfloat16)

    def out_product(part):
        return jnp.dot(part, out_weight, preferred_element_type=jnp.float32)

    resid = inputs + summed_rows(out_product, attended)
    normed_two, unit_two, scale_two = layer_norm(resid, norm_gains[1], norm_biases[1])
    normed_two_low = normed_two.astype(jnp.bfloat16)
    normed_two_all = gather_rows(normed_two_low)
    two_four = lax.all_gather(normed_two_low, ("grp", "seq"), axis=0, tiled=True)

    def up_to_back(two, up):
        gate_up = jnp.einsum("td,dcf->tcf", two, gate_up_weight, preferred_element_type=jnp.float32)
        hidden, gate, upper, sigma = silu_parts(gate_up)
        hidden_back = jnp.einsum("td,fd->tf", up, down_weight, preferred_element_type=jnp.float32)
        return hidden.astype(jnp.bfloat16), gate_back(hidden_back, gate, upper, sigma)

    hidden_low, gate_up_back = up_to_back(normed_two_all, upstream_all)

    def down_product(part):
        return jnp.dot(part, down_weight, preferred_element_type=jnp.float32)

    layer_out = resid + summed_rows(down_product, hidden_low)

    def gate_up_product(part):
        return jnp.einsum("tcf,dcf->td", part, gate_up_weight, preferred_element_type=jnp.float32)

    normed_two_back = summed_rows(gate_up_product, gate_up_back)
    hidden_four, back_four = up_to_back(two_four, up_four)
    down_grad = jnp.einsum("tf,td->fd", hidden_four, up_four, preferred_element_type=jnp.float32)
    gate_up_grad = jnp.einsum(
        "td,tcf->dcf", two_four, back_four, preferred_element_type=jnp.float32
    )
    resid_part, gain_two, bias_two = norm_back(normed_two_back, unit_two, scale_two, norm_gains[1])
    resid_back = upstream + resid_part
    branch_all = gather_rows(resid_back.astype(jnp.bfloat16))
    out_term = jnp.einsum("te,td->ed", attended, branch_all, preferred_element_type=jnp.float32)
    out_grad = lax.psum(out_term.astype(jnp.bfloat16), "grp").astype(jnp.float32)
    attended_back = jnp.einsum(
        "td,ed->te", branch_all, out_weight, preferred_element_type=jnp.float32
    ).astype(jnp.bfloat16)
    heads_back = attended_back.reshape(group_slots, local_heads, HEAD_DIM)
    query_back, key_back, value_back = attend_back(
        query, key, value, label_all, log_totals, heads_back, block
    )
    lowered = jnp.stack([query_back, key_back, value_back], axis=1).astype(jnp.bfloat16)
    mixin_back = unrotate(lowered, place_all)
    mix_term = jnp.einsum("td,tcf->dcf", normed_all, mixin_back, preferred_element_type=jnp.float32)
    mix_grad = lax.psum(mix_term.astype(jnp.bfloat16), "grp").astype(jnp.float32)
    bias_term = jnp.sum(mixin_back, axis=0, dtype=jnp.float32)
    mix_bias_grad = lax.psum(bias_term, "grp")

    def mix_product(part):
        return jnp.einsum("tcf,dcf->td", part, mix_weight, preferred_element_type=jnp.float32)

    normed_back = summed_rows(mix_product, mixin_back)
    tokens_part, gain_one, bias_one = norm_back(normed_back, unit_one, scale_one, norm_gains[0])
    tokens_grad = (resid_back + tokens_part).astype(jnp.bfloat16)
    gains_grad, biases_grad = lax.psum(
        (jnp.stack([gain_one, gain_two]), jnp.stack([bias_one, bias_two])), ("grp", "seq")
    )
    return (
        layer_out.astype(jnp.bfloat16),
        tokens_grad,
        gains_grad,
        biases_grad,
        mix_grad,
        mix_bias_grad,
        out_grad,
        gate_up_grad,
        down_grad,
    )


MESH_ID = pl.DeviceIdType.MESH
N_RS = 10
N_AG = 13


class Ring:
    def __init__(self):
        self.group = lax.axis_index("grp")
        self.me = lax.axis_index("seq")
        core = self.me % 2
        x = (self.me // 2) % 2
        y = self.me // 4
        self.flip = 1 - 2 * core
        self.twin = self.me + self.flip
        self.xn = self.me + 2 - 4 * x
        self.yn = self.me + 4 - 8 * y
        self.dn = self.xn + 4 - 8 * y

    def dev(self, seq):
        return (self.group, seq)

    def greet(self, extra=()):
        sem = pltpu.get_barrier_semaphore()
        peers = [self.dev(self.twin), self.dev(self.xn), self.dev(self.yn)] + list(extra)
        for peer in peers:
            pl.semaphore_signal(sem, inc=1, device_id=peer, device_id_type=MESH_ID)
        return lambda: pl.semaphore_wait(sem, len(peers))

    def barrier(self, extra=()):
        self.greet(extra)()

    def chips(self):
        return [self.dn // 2, self.xn // 2, self.yn // 2, self.me // 2]

    def copy(self, src, dst, send, recv, kind, seq):
        return pltpu.make_async_remote_copy(
            src_ref=src,
            dst_ref=dst,
            send_sem=send.at[kind],
            recv_sem=recv.at[kind],
            device_id=self.dev(seq),
            device_id_type=MESH_ID,
        )


class Line:
    def __init__(self, ring, send, recv):
        self.ring, self.send, self.recv = ring, send, recv
        self.groups = lax.axis_size("grp")
        self.peers = [(self.away(k), ring.me) for k in range(1, self.groups)]

    def away(self, k):
        return lax.rem(self.ring.group + k, self.groups)

    def copy(self, k, src, dst):
        return pltpu.make_async_remote_copy(
            src_ref=src,
            dst_ref=dst,
            send_sem=self.send.at[k - 1],
            recv_sem=self.recv.at[k - 1],
            device_id=self.peers[k - 1],
            device_id_type=MESH_ID,
        )


def line_sems():
    return [pltpu.SemaphoreType.DMA((lax.axis_size("grp"),)), pltpu.SemaphoreType.DMA((lax.axis_size("grp"),))]


class Gather:
    def __init__(self, ring, own, out, send, recv, local):
        self.ring, self.own, self.out = ring, own, out
        self.send, self.recv, self.local = send, recv, local
        self.rows = own.shape[0]
        self.half = self.rows // 2

    def at(self, block, part=None):
        rows, half = self.rows, self.half
        if part is None:
            return self.out.at[pl.ds(pl.multiple_of(block * rows, rows), rows), :]
        return self.out.at[pl.ds(pl.multiple_of(block * rows + part * half, half), half), :]

    def copy(self, kind):
        ring, half = self.ring, self.half
        if kind < 4:
            part, seq = ((0, ring.xn), (1, ring.yn), (1, ring.xn), (0, ring.yn))[kind]
            src, dst = self.own.at[pl.ds(part * half, half), :], self.at(ring.me, part)
        elif kind == 4:
            src, dst, seq = self.own, self.at(ring.me), ring.twin
        else:
            block, part, seq = (
                (ring.xn, 0, ring.yn),
                (ring.xn, 0, ring.twin),
                (ring.yn, 1, ring.xn),
                (ring.yn, 1, ring.twin),
                (ring.xn, 1, ring.twin),
                (ring.yn, 0, ring.twin),
                (ring.dn, 0, ring.twin),
                (ring.dn, 1, ring.twin),
            )[kind - 5]
            src = dst = self.at(block, part)
        return ring.copy(src, dst, self.send, self.recv, kind, seq)

    def keep(self):
        return pltpu.make_async_copy(self.own, self.at(self.ring.me), self.local)

    def stage(self, number):
        if number == 0:
            self.keep().start()
            for kind in range(5):
                self.copy(kind).start()
        elif number == 1:
            self.copy(0).wait_recv()
            self.copy(5).start()
            self.copy(6).start()
            self.copy(1).wait_recv()
            self.copy(7).start()
            self.copy(8).start()
        elif number == 2:
            self.copy(2).wait_recv()
            self.copy(9).start()
            self.copy(3).wait_recv()
            self.copy(10).start()
        elif number == 3:
            self.copy(5).wait_recv()
            self.copy(11).start()
            self.copy(7).wait_recv()
            self.copy(12).start()
        else:
            self.arrive(4, 6, 8, 9, 10, 11, 12)
            self.close()

    def arrive(self, *kinds):
        for kind in kinds:
            self.copy(kind).wait_recv()

    def close_sends(self):
        for kind in range(N_AG):
            self.copy(kind).wait_send()

    def close(self):
        self.keep().wait()
        self.close_sends()

    def all(self):
        for number in range(5):
            self.stage(number)


class Scatter:
    def __init__(self, ring, part, total, own, pair, rx, ry, fx, fy, mid, send, recv, local):
        self.ring, self.part, self.total = ring, part, total
        self.own, self.pair, self.rx, self.ry = own, pair, rx, ry
        self.fx, self.fy, self.mid = fx, fy, mid
        self.send, self.recv, self.local = send, recv, local
        self.rows, self.width = total.shape

    def block(self, index):
        return self.part.at[pl.ds(pl.multiple_of(index * self.rows, self.rows), self.rows), :]

    def index(self, slot):
        ring = self.ring
        return (ring.dn, ring.xn, ring.yn, ring.me)[slot]

    def keep(self, slot):
        return pltpu.make_async_copy(self.block(self.index(slot)), self.own.at[slot], self.local.at[slot])

    def copy(self, kind):
        ring, half = self.ring, self.width // 2
        lo, hi = pl.ds(0, half), pl.ds(half, half)
        if kind < 4:
            src, dst, seq = self.block(self.index(kind) + ring.flip), self.pair.at[kind], ring.twin
        else:
            src, dst, seq = (
                (self.own.at[0, :, lo], self.rx.at[0], ring.xn),
                (self.own.at[0, :, hi], self.ry.at[0], ring.yn),
                (self.own.at[1, :, lo], self.rx.at[1], ring.xn),
                (self.own.at[2, :, hi], self.ry.at[1], ring.yn),
                (self.mid.at[0], self.fy, ring.yn),
                (self.mid.at[1], self.fx, ring.xn),
            )[kind - 4]
        return ring.copy(src, dst, self.send, self.recv, kind, seq)

    def added(self, slot):
        self.keep(slot).wait()
        self.copy(slot).wait_recv()
        return self.own[slot].astype(jnp.float32) + self.pair[slot].astype(jnp.float32)

    def stage(self, number):
        wide, low, half = jnp.float32, self.own.dtype, self.width // 2
        lo, hi = pl.ds(0, half), pl.ds(half, half)
        own, total = self.own, self.total
        if number == 0:
            for slot in range(4):
                self.copy(slot).start()
                self.keep(slot).start()
        elif number == 1:
            own[0] = self.added(0).astype(low)
            self.copy(4).start()
            self.copy(5).start()
            own[1] = self.added(1).astype(low)
            self.copy(6).start()
            own[2] = self.added(2).astype(low)
            self.copy(7).start()
            total[...] = self.added(3)
        elif number == 2:
            self.copy(4).wait_recv()
            self.mid[0] = (own[2, :, lo].astype(wide) + self.rx[0].astype(wide)).astype(low)
            self.copy(8).start()
            self.copy(5).wait_recv()
            self.mid[1] = (own[1, :, hi].astype(wide) + self.ry[0].astype(wide)).astype(low)
            self.copy(9).start()
        else:
            self.copy(6).wait_recv()
            total[:, lo] += self.rx[1].astype(wide)
            self.copy(7).wait_recv()
            total[:, hi] += self.ry[1].astype(wide)
            self.copy(8).wait_recv()
            total[:, lo] += self.fy[...].astype(wide)
            self.copy(9).wait_recv()
            total[:, hi] += self.fx[...].astype(wide)
            for kind in range(N_RS):
                self.copy(kind).wait_send()

    def all(self):
        for number in range(4):
            self.stage(number)


class Stream:
    def __init__(self, ring, tiles, total, pair, rx, ry, fx, fy, mid, send, recv):
        self.ring, self.tiles, self.total, self.pair = ring, tiles, total, pair
        self.rx, self.ry, self.fx, self.fy, self.mid = rx, ry, fx, fy, mid
        self.send, self.recv = send, recv
        self.rows, self.width = total.shape
        self.at = ring.chips()

    def rows_of(self, twin):
        core = self.ring.me % 2
        core = 1 - core if twin else core
        return pl.ds(pl.multiple_of(core * self.rows, self.rows), self.rows)

    def copy(self, kind):
        ring, half = self.ring, self.width // 2
        lo, hi = pl.ds(0, half), pl.ds(half, half)
        mine = self.rows_of(False)
        dn, xn, yn, _ = self.at
        src, dst, seq = (
            (self.tiles.at[dn, mine, lo], self.rx.at[0], ring.xn),
            (self.tiles.at[dn, mine, hi], self.ry.at[0], ring.yn),
            (self.tiles.at[xn, mine, lo], self.rx.at[1], ring.xn),
            (self.tiles.at[yn, mine, hi], self.ry.at[1], ring.yn),
            (self.mid.at[0], self.fy, ring.yn),
            (self.mid.at[1], self.fx, ring.xn),
        )[kind - 4]
        return ring.copy(src, dst, self.send, self.recv, kind, seq)

    def pair_copy(self, chip):
        return self.ring.copy(
            self.tiles.at[chip, self.rows_of(True), :],
            self.pair.at[chip],
            self.send,
            self.recv,
            chip,
            self.ring.twin,
        )

    def ready(self, chip):
        self.pair_copy(chip).start()

    def added(self, chip):
        self.pair_copy(chip).wait_recv()
        mine = self.rows_of(False)
        return self.tiles[chip, mine, :].astype(jnp.float32) + self.pair[chip].astype(jnp.float32)

    def go(self, which):
        chip = self.at[which]
        self.tiles[chip, self.rows_of(False), :] = self.added(chip).astype(self.tiles.dtype)
        for kind in ((4, 5), (6,), (7,))[which]:
            self.copy(kind).start()

    def cross(self):
        wide, low, half = jnp.float32, self.tiles.dtype, self.width // 2
        lo, hi = pl.ds(0, half), pl.ds(half, half)
        mine = self.rows_of(False)
        _, xn, yn, _ = self.at
        self.copy(4).wait_recv()
        self.mid[0] = (self.tiles[yn, mine, lo].astype(wide) + self.rx[0].astype(wide)).astype(low)
        self.copy(8).start()
        self.copy(5).wait_recv()
        self.mid[1] = (self.tiles[xn, mine, hi].astype(wide) + self.ry[0].astype(wide)).astype(low)
        self.copy(9).start()

    def finish(self):
        wide, half = jnp.float32, self.width // 2
        lo, hi = pl.ds(0, half), pl.ds(half, half)
        total = self.total
        total[...] = self.added(self.at[3])
        self.copy(6).wait_recv()
        total[:, lo] += self.rx[1].astype(wide)
        self.copy(7).wait_recv()
        total[:, hi] += self.ry[1].astype(wide)
        self.copy(8).wait_recv()
        total[:, lo] += self.fy[...].astype(wide)
        self.copy(9).wait_recv()
        total[:, hi] += self.fx[...].astype(wide)

    def close(self):
        for chip in range(4):
            self.pair_copy(chip).wait_send()
        for kind in range(4, N_RS):
            self.copy(kind).wait_send()


def stream_scratch(rows, width):
    low = jnp.bfloat16
    half = width // 2
    return [
        pltpu.VMEM((4, 2 * rows, width), low),
        pltpu.VMEM((rows, width), jnp.float32),
        pltpu.VMEM((4, rows, width), low),
        pltpu.VMEM((2, rows, half), low),
        pltpu.VMEM((2, rows, half), low),
        pltpu.VMEM((rows, half), low),
        pltpu.VMEM((rows, half), low),
        pltpu.VMEM((2, rows, half), low),
        pltpu.SemaphoreType.DMA((N_RS,)),
        pltpu.SemaphoreType.DMA((N_RS,)),
    ]


N_STREAM = 10


def scatter_buffers(rows, width):
    low = jnp.bfloat16
    half = width // 2
    return [
        pltpu.VMEM((rows, width), jnp.float32),
        pltpu.VMEM((4, rows, width), low),
        pltpu.VMEM((4, rows, width), low),
        pltpu.VMEM((2, rows, half), low),
        pltpu.VMEM((2, rows, half), low),
        pltpu.VMEM((rows, half), low),
        pltpu.VMEM((rows, half), low),
        pltpu.VMEM((2, rows, half), low),
    ]


def scatter_sems():
    return [
        pltpu.SemaphoreType.DMA((N_RS,)),
        pltpu.SemaphoreType.DMA((N_RS,)),
        pltpu.SemaphoreType.DMA((4,)),
    ]


def scatter_scratch(rows, width):
    return scatter_buffers(rows, width) + scatter_sems()


def gather_sems():
    return [
        pltpu.SemaphoreType.DMA((N_AG,)),
        pltpu.SemaphoreType.DMA((N_AG,)),
        pltpu.SemaphoreType.DMA,
    ]


def gather_scratch(rows, width):
    return [pltpu.VMEM((rows, width), jnp.bfloat16)] + gather_sems()


def unit_of(values):
    centered = values - jnp.mean(values, axis=-1, keepdims=True)
    scale = lax.rsqrt(jnp.mean(centered * centered, axis=-1, keepdims=True) + EPS)
    return centered * scale, scale


def back_of(incoming, unit, scale, gain):
    along = incoming * gain
    inner = jnp.mean(along, axis=-1, keepdims=True)
    cross = jnp.mean(along * unit, axis=-1, keepdims=True)
    return scale * (along - inner - unit * cross)


VM = pl.BlockSpec(memory_space=pltpu.VMEM)
ANY = pl.BlockSpec(memory_space=pltpu.HBM)
SM = pl.BlockSpec(memory_space=pltpu.SMEM)


def call(kernel, number, ins, outs, scratch, limit=60, flops=0, cost=20_000_000, scratch_in=None):
    return pl.pallas_call(
        kernel,
        out_shape=tuple(jax.ShapeDtypeStruct(*shape) for shape, _ in outs),
        in_specs=[spec for _, spec in ins],
        out_specs=tuple(spec for _, spec in outs),
        scratch_shapes=scratch,
        compiler_params=pltpu.CompilerParams(
            collective_id=number,
            has_side_effects=True,
            vmem_limit_bytes=limit << 20,
        ),
        cost_estimate=pl.CostEstimate(flops=flops, bytes_accessed=cost, transcendentals=0),
    )(*[value for value, _ in ins])


TILE = 256
WIDE = jnp.float32
LOW = jnp.bfloat16
NT = (((1,), (1,)), ((), ()))
TN = (((0,), (0,)), ((), ()))


def mm(a, b, dims=(((1,), (0,)), ((), ()))):
    return lax.dot_general(a, b, dims, preferred_element_type=WIDE)


def far_rows(far, ring, away, total):
    groups = lax.axis_size("grp")
    rows = far.shape[0] // groups
    index = lax.rem(ring.group + away, groups)
    return far.at[pl.ds(pl.multiple_of(index * rows, rows), rows), :]


def head_lanes(shape, head):
    return lax.broadcasted_iota(jnp.int32, shape, 1) // HEAD_DIM == head


def turn(u, tables, rows, sign):
    cosine, below, above = (
        jnp.concatenate([tables[i, rows, :]] * (u.shape[1] // 128), axis=1) for i in range(3)
    )
    side = pltpu.roll(u, 8, 1) * below + pltpu.roll(u, u.shape[1] - 8, 1) * above
    return u * cosine + side if sign > 0 else u * cosine - side


def load(pairs, sems):
    copies = []
    for i, (src, dst) in enumerate(pairs):
        copy = pltpu.make_async_copy(src, dst, sems.at[i])
        copy.start()
        copies.append(copy)
    return copies


def rows_layout(row_lengths, row_group, group, tables, lab_col, lab_row):
    total = lab_col.shape[0]
    rows, begin = [], jnp.int32(0)
    for row in range(row_lengths.shape[0]):
        mine = row_group[row] == group
        rows.append((row, mine, begin, begin + row_lengths[row]))
        begin = begin + jnp.where(mine, row_lengths[row], 0)

    def lay(slots):
        label, base = jnp.full(slots.shape, -1, jnp.int32), jnp.full(slots.shape, begin, jnp.int32)
        for row, mine, first, end in rows:
            first, end = jnp.where(mine, first, -1), jnp.where(mine, end, -1)
            inside = (slots >= first) & (slots < end)
            label = jnp.where(inside, row, label)
            base = jnp.where(inside, first, base)
        return label, slots - base

    lab_row[...] = lay(lax.broadcasted_iota(jnp.int32, (1, total), 1))[0]
    half = ROT // 2

    def body(i, carry):
        at = pl.ds(pl.multiple_of(i * TILE, TILE), TILE)
        label, place = lay(i * TILE + lax.broadcasted_iota(jnp.int32, (TILE, 1), 0))
        lab_col[at, :] = label
        lane = lax.broadcasted_iota(jnp.int32, (TILE, 128), 1) % HEAD_DIM
        freq = jnp.ones((TILE, 128), WIDE)
        for e in range(1, half):
            freq = jnp.where(lane % half == e, BASE ** (-e / half), freq)
        angle = place.astype(WIDE) * freq
        cosine, sine = jnp.cos(angle), jnp.sin(angle)
        tables[0, at, :] = jnp.where(lane < ROT, cosine, 1.0)
        tables[1, at, :] = jnp.where((lane >= half) & (lane < ROT), sine, 0.0)
        tables[2, at, :] = jnp.where(lane < half, -sine, 0.0)
        return carry

    lax.fori_loop(0, total // TILE, body, 0)


def attend_kernel(
    row_lengths, row_group, tokens, gains, biases, upstream, weight, out_weight, bias,
    query, key, value, attended, lse, normed_all, up_all, resid, two_all, two_own, tables, lab_col, lab_row,
    normed, own, w, mask, stats, sems, *scratch,
):
    total, width = query.shape
    tiles = total // TILE
    ring = Ring()
    met = ring.greet()
    copy_w = pltpu.make_async_copy(weight, w, sems.at[0])
    copy_w.start()
    stream = Stream(ring, *scratch[:N_STREAM])
    scratch = scratch[N_STREAM:]
    gather = Gather(ring, own, normed, *scratch[0:3])
    upper = Gather(ring, upstream, up_all, *scratch[3:6])
    after = Gather(ring, two_own, two_all, *scratch[6:9])
    unit, _ = unit_of(tokens[...].astype(WIDE))
    own[...] = (unit * gains[0:1] + biases[0:1]).astype(LOW)
    met()
    gather.stage(0)
    rows_layout(row_lengths, row_group, ring.group, tables, lab_col, lab_row)
    gather.keep().wait()
    copy_w.wait()

    def mix(chip):
        rows = pl.ds(pl.multiple_of(chip * TILE, TILE), TILE)
        x = normed[rows, :]
        u = mm(x, w[0]) + bias[0:1].astype(WIDE)
        query[rows, :] = (turn(u, tables, rows, 1).astype(LOW).astype(WIDE) * (1.0 / 8)).astype(LOW)
        u = mm(x, w[1]) + bias[1:2].astype(WIDE)
        key[rows, :] = turn(u, tables, rows, 1).astype(LOW)
        value[rows, :] = (mm(x, w[2]) + bias[2:3].astype(WIDE)).astype(LOW)

    chips = ring.chips()

    def mix_body(step, carry):
        for i, acts in enumerate(
            (
                ((4,), ()),
                ((6, 9), (1, 2)),
                ((8, 10), (3,)),
                ((11, 12), ()),
            )
        ):

            @pl.when(step == i)
            def _():
                for number in acts[1]:
                    gather.stage(number)
                if i == 2:
                    upper.stage(0)
                gather.arrive(*acts[0])

        chip = chips[0]
        for i in range(1, tiles):
            chip = jnp.where(step == tiles - 1 - i, chips[(3, 1, 2)[tiles - 1 - i]], chip)
        mix(chip)
        return carry

    lax.fori_loop(0, tiles, mix_body, 0)
    keep = pltpu.make_async_copy(normed, normed_all, sems.at[1])
    keep.start()
    for i in range(tiles):
        rows = pl.ds(i * TILE, TILE)
        span = (i + 1) * TILE
        q_at = i * TILE + lax.broadcasted_iota(jnp.int32, (TILE, span), 0)
        k_at = lax.broadcasted_iota(jnp.int32, (TILE, span), 1)
        allowed = (lab_col[rows, :] == lab_row[:, :span]) & (q_at >= k_at)
        mask[:, :span] = jnp.where(allowed, 0.0, NEG)
        q = query[rows, :]

        def one_head(head, carry):
            mixed, logs = carry
            mine = head_lanes(q.shape, head)
            s = mm(jnp.where(mine, q, jnp.zeros_like(q)), key[:span, :], NT) + mask[:, :span]
            top = jnp.max(s, axis=1, keepdims=True)
            p = jnp.exp(s - top)
            norm = jnp.sum(p, axis=1, keepdims=True)
            o = mm(p.astype(LOW), value[:span, :]) / norm
            mixed = jnp.where(mine, o, mixed)
            lane = lax.broadcasted_iota(jnp.int32, logs.shape, 1)
            logs = jnp.where(lane == head, top + jnp.log(norm), logs)
            return mixed, logs

        mixed, logs = lax.fori_loop(
            0, width // HEAD_DIM, one_head,
            (jnp.zeros((TILE, width), WIDE), jnp.zeros((TILE, 128), WIDE)),
        )
        low = mixed.astype(LOW)
        attended[rows, :] = low
        stats[rows, :] = logs
        stream.tiles[i] = mm(low, out_weight[...]).astype(LOW)
        stream.ready(i)
        if i >= 1:
            upper.stage(i)
    for which in range(3):
        stream.go(which)
    lse[...] = jnp.transpose(stats[...])[:8, :]
    stream.cross()
    stream.finish()
    resid[...] = stream.total[...] + tokens[...].astype(WIDE)
    unit, _ = unit_of(resid[...])
    two_own[...] = (unit * gains[1:2] + biases[1:2]).astype(LOW)
    after.all()
    upper.stage(4)
    gather.close_sends()
    stream.close()
    keep.wait()


def attend_heads(
    row_lengths, row_group, tokens, gains, biases, upstream, weight, out_weight, bias, count
):
    rows, width = tokens.shape
    total = rows * count
    local = out_weight.shape[0]
    slab = (((total, local), LOW), VM)
    tall = (((total, width), LOW), ANY)
    return call(
        attend_kernel,
        5,
        [(row_lengths, SM), (row_group, SM), (tokens, VM), (gains, VM), (biases, VM), (upstream, VM)]
        + [(weight, ANY), (out_weight, VM), (bias, VM)],
        [
            slab, slab, slab, slab,
            (((8, total), WIDE), VM),
            tall,
            tall,
            (((rows, width), WIDE), VM),
            tall,
            (((rows, width), LOW), VM),
            (((3, total, 128), WIDE), VM),
            (((total, 1), jnp.int32), VM),
            (((1, total), jnp.int32), VM),
        ],
        [
            pltpu.VMEM((total, width), LOW),
            pltpu.VMEM((rows, width), LOW),
            pltpu.VMEM((3, width, local), LOW),
            pltpu.VMEM((TILE, total), WIDE),
            pltpu.VMEM((total, 128), WIDE),
            pltpu.SemaphoreType.DMA((2,)),
        ]
        + stream_scratch(rows, width)
        + gather_sems() * 3,
        limit=60,
        flops=7 << 30,
    )


def attend_back_kernel(
    branch_all, normed_all, out_weight, tables, lab_col, lab_row,
    query, key, value, attended, lse, far,
    mixin_out, terms, out_sum, bias_term, far_all,
    branch, normed, mask, inner, heads_back, query_back, key_back, value_back, mixin, mixes,
    sems, outs, out_term, out_inbox, *scratch,
):
    total, width = query.shape
    tiles = total // TILE
    heads = width // HEAD_DIM
    ring = Ring()
    line = Line(ring, *scratch[3:5])
    ring.barrier(line.peers)
    gather = Gather(ring, far_rows(far, ring, 1, total), far_all, *scratch[0:3])
    share = out_term.shape[0] // line.groups

    def share_of(group):
        return pl.ds(pl.multiple_of(group * share, share), share)

    def out_copy(k):
        return line.copy(k, out_term.at[share_of(line.away(k)), :], out_inbox.at[k - 1])

    gather.stage(0)
    loads = load(
        [(branch_all.at[pl.ds(i * TILE, TILE), :], branch.at[pl.ds(i * TILE, TILE), :]) for i in range(tiles)]
        + [(normed_all, normed)],
        sems,
    )
    head_of = lax.broadcasted_iota(jnp.int32, (8, width), 1) // HEAD_DIM
    pick = (head_of == lax.broadcasted_iota(jnp.int32, (8, width), 0)).astype(LOW)
    for i in range(tiles):
        rows = pl.ds(i * TILE, TILE)
        loads[i].wait()
        low = mm(branch[rows, :], out_weight[...], NT).astype(LOW)
        heads_back[rows, :] = low
        prod = low.astype(WIDE) * attended[rows, :].astype(WIDE)
        high = prod.astype(LOW)
        rest = (prod - high.astype(WIDE)).astype(LOW)
        inner[:, rows] = mm(pick, high, NT) + mm(pick, rest, NT)
    out_term[...] = mm(attended[...], branch[...], TN).astype(LOW)
    for k in range(1, line.groups):
        out_copy(k).start()
    gather.stage(1)
    key_back[...] = jnp.zeros_like(key_back)
    value_back[...] = jnp.zeros_like(value_back)
    for i in range(tiles):
        rows = pl.ds(i * TILE, TILE)
        span = (i + 1) * TILE
        k_at = lax.broadcasted_iota(jnp.int32, (span, TILE), 0)
        q_at = i * TILE + lax.broadcasted_iota(jnp.int32, (span, TILE), 1)
        allowed = (lab_col[:span, :] == lab_row[:, rows]) & (q_at >= k_at)
        mask[:span, :] = jnp.where(allowed, 0.0, NEG)
        q = query[rows, :]
        d_out = heads_back[rows, :]

        def one_head(head, q_back):
            mine = head_lanes(q.shape, head)
            q_h = jnp.where(mine, q, jnp.zeros_like(q))
            d_h = jnp.where(mine, d_out, jnp.zeros_like(q))
            k = key[:span, :]
            k_h = jnp.where(head_lanes(k.shape, head), k, jnp.zeros_like(k))
            p = jnp.exp(mm(k, q_h, NT) + mask[:span, :] - lse[pl.ds(head, 1), rows])
            d_p = mm(value[:span, :], d_h, NT)
            d_s = (p * (d_p - inner[pl.ds(head, 1), rows])).astype(LOW)
            value_back[:span, :] += mm(p.astype(LOW), d_h)
            key_back[:span, :] += mm(d_s, q_h)
            return q_back + mm(d_s, k_h, TN)

        query_back[rows, :] = lax.fori_loop(0, heads, one_head, jnp.zeros((TILE, width), WIDE))
        if i >= 2:
            gather.stage(i)
    loads[-1].wait()
    copies = []
    sums = [jnp.zeros((1, width), WIDE)] * 3
    for i in range(tiles):
        rows = pl.ds(i * TILE, TILE)
        q_b = (query_back[rows, :] * (1.0 / 8)).astype(LOW).astype(WIDE)
        k_b = key_back[rows, :].astype(LOW).astype(WIDE)
        trio = [
            turn(q_b, tables, rows, -1).astype(LOW),
            turn(k_b, tables, rows, -1).astype(LOW),
            value_back[rows, :].astype(LOW),
        ]
        for c, item in enumerate(trio):
            mixin[c, rows, :] = item
            sums[c] = sums[c] + jnp.sum(item.astype(WIDE), axis=0, keepdims=True)
    copy = pltpu.make_async_copy(mixin, mixin_out, outs.at[3])
    copy.start()
    copies.append(copy)
    for c in range(3):
        bias_term[c : c + 1, :] = sums[c]
        mixes[c] = mm(normed[...], mixin[c], TN).astype(LOW)
        copy = pltpu.make_async_copy(mixes.at[c], terms.at[c], outs.at[c])
        copy.start()
        copies.append(copy)
    summed = out_term[share_of(ring.group), :].astype(WIDE)
    for k in range(1, line.groups):
        out_copy(k).wait_recv()
        summed = summed + out_inbox[k - 1].astype(WIDE)
    out_sum[...] = summed.astype(LOW)
    gather.stage(4)
    for k in range(1, line.groups):
        out_copy(k).wait_send()
    for copy in copies:
        copy.wait()


def attend_heads_back(
    branch_all, normed_all, out_weight, tables, lab_col, lab_row, saved, far
):
    total, width = normed_all.shape
    local = out_weight.shape[0]
    tiles = total // TILE
    groups = lax.axis_size("grp")
    tall = (((total, width), LOW), ANY)
    return call(
        attend_back_kernel,
        6,
        [(item, ANY) for item in (branch_all, normed_all)]
        + [(item, VM) for item in (out_weight, tables, lab_col, lab_row) + tuple(saved)]
        + [(far, ANY)],
        [
            (((3, total, local), LOW), ANY),
            (((3, width, local), LOW), ANY),
            (((local // groups, width), LOW), VM),
            (((3, local), WIDE), VM),
            tall,
        ],
        [
            pltpu.VMEM((total, width), LOW),
            pltpu.VMEM((total, width), LOW),
            pltpu.VMEM((total, TILE), WIDE),
            pltpu.VMEM((8, total), WIDE),
            pltpu.VMEM((total, local), LOW),
            pltpu.VMEM((total, local), WIDE),
            pltpu.VMEM((total, local), WIDE),
            pltpu.VMEM((total, local), WIDE),
            pltpu.VMEM((3, total, local), LOW),
            pltpu.VMEM((3, width, local), LOW),
            pltpu.SemaphoreType.DMA((tiles + 1,)),
            pltpu.SemaphoreType.DMA((4,)),
            pltpu.VMEM((local, width), LOW),
            pltpu.VMEM((groups - 1, local // groups, width), LOW),
        ]
        + gather_sems()
        + line_sems(),
        limit=60,
        flops=16 << 30,
    )


def units(gate, upper, hidden_back):
    sigma = jax.nn.sigmoid(gate)
    silu = gate * sigma
    return (
        (silu * upper).astype(LOW),
        (hidden_back * (upper * (sigma + silu * (1.0 - sigma)))).astype(LOW),
        (hidden_back * silu).astype(LOW),
    )


def forward_units(two, up, wide, down):
    return units(mm(wide[0], two, NT), mm(wide[1], two, NT), mm(down[...], up, NT))


def feed_kernel(
    two_all, up_all, wide_hbm, down_hbm, far, resid, upstream, gains,
    down_part, saved, far_one, resid_back, branch_all, sums,
    two, up, wide, down, kept, stage, own, sems, outs, *scratch,
):
    total = two_all.shape[0]
    tiles = total // TILE
    ring = Ring()
    met = ring.greet()
    stream = Stream(ring, *scratch[:N_STREAM])
    gather = Gather(ring, far_rows(far, ring, 1, total), far_one, *scratch[N_STREAM : N_STREAM + 3])
    branch = Gather(ring, own, branch_all, *scratch[N_STREAM + 3 :])
    chips = ring.chips()

    def rows_of(chip):
        return pl.ds(pl.multiple_of(chip * TILE, TILE), TILE)

    def tile_loads(step, chip):
        return [
            pltpu.make_async_copy(two_all.at[rows_of(chip), :], two.at[step], sems.at[0, step]),
            pltpu.make_async_copy(up_all.at[rows_of(chip), :], up.at[step], sems.at[1, step]),
        ]

    weights = load([(wide_hbm, wide), (down_hbm, down)], sems.at[2])
    for step in range(tiles):
        for copy in tile_loads(step, chips[step]):
            copy.start()
    met()
    gather.stage(0)
    for copy in weights:
        copy.wait()

    def chip_at(step):
        chip = chips[tiles - 1]
        for i in range(tiles - 1):
            chip = jnp.where(step == i, chips[i], chip)
        return chip

    def body(step, carry):
        chip = chip_at(step)
        for copy in tile_loads(step, chip):
            copy.wait()
        trio = forward_units(two[step], up[step], wide, down)
        for c in range(3):
            kept[c, :, rows_of(chip)] = trio[c]
        for i in range(1, tiles):

            @pl.when(step == i)
            def _():
                stream.go(i - 1)
                if i == tiles - 1:
                    stream.cross()

        stream.tiles[chip] = (mm(trio[1], wide[0], TN) + mm(trio[2], wide[1], TN)).astype(LOW)
        stream.ready(chip)
        for i in range(tiles):

            @pl.when(step == i)
            def _():
                if i < 3:
                    gather.stage(i + 1)

        return carry

    lax.fori_loop(0, tiles, body, 0)
    keep = pltpu.make_async_copy(kept, saved, outs.at[tiles])
    keep.start()
    unit, scale = unit_of(resid[...])
    stream.finish()
    incoming = stream.total[...]
    back = upstream[...].astype(WIDE) + back_of(incoming, unit, scale, gains[1:2])
    resid_back[...] = back
    own[...] = back.astype(LOW)
    branch.stage(0)
    sums[0:1] = jnp.sum(incoming * unit, axis=0, keepdims=True)
    sums[1:2] = jnp.sum(incoming, axis=0, keepdims=True)

    def down_copy(i):
        start = i * TILE if isinstance(i, int) else pl.multiple_of(i * TILE, TILE)
        rows = pl.ds(start, TILE)
        return pltpu.make_async_copy(stage.at[i], down_part.at[rows, :], outs.at[i])

    def down_body(i, carry):
        stage[i] = mm(kept[0, :, rows_of(i)], down[...], TN).astype(LOW)
        down_copy(i).start()
        for number in (1, 2, 3):

            @pl.when(i == number)
            def _():
                branch.stage(number)

        return carry

    lax.fori_loop(0, tiles, down_body, 0)
    branch.stage(4)
    gather.stage(4)
    stream.close()
    keep.wait()
    for i in range(tiles):
        down_copy(i).wait()


def feed(two_all, up_all, wide, down, far, resid, upstream, gains):
    total, width = two_all.shape
    rows = resid.shape[0]
    local = down.shape[0]
    tiles = total // TILE
    tall = (((total, width), LOW), ANY)
    return call(
        feed_kernel,
        7,
        [(item, ANY) for item in (two_all, up_all, wide, down, far)]
        + [(item, VM) for item in (resid, upstream, gains)],
        [
            tall,
            (((3, local, total), LOW), ANY),
            tall,
            (((rows, width), WIDE), VM),
            tall,
            (((2, width), WIDE), VM),
        ],
        [
            pltpu.VMEM((tiles, TILE, width), LOW),
            pltpu.VMEM((tiles, TILE, width), LOW),
            pltpu.VMEM((2, local, width), LOW),
            pltpu.VMEM((local, width), LOW),
            pltpu.VMEM((3, local, total), LOW),
            pltpu.VMEM((tiles, TILE, width), LOW),
            pltpu.VMEM((rows, width), LOW),
            pltpu.SemaphoreType.DMA((3, tiles)),
            pltpu.SemaphoreType.DMA((1 + tiles,)),
        ]
        + stream_scratch(rows, width)
        + gather_sems() * 2,
        limit=60,
        flops=18 << 30,
    )


N_LAST_GATHERS = 4


def last_kernel(
    mix_part, down_part, tokens, resid, resid_back, gains, sums, bias_term, out_sum,
    two_all, up_all, saved, two_far, up_far, up_one, two_one, wide_hbm, down_hbm,
    tokens_grad, layer_out, four, out_grad, wide_grad, down_grad, two_two, two_three, up_two, up_three,
    two, up, kept, wide, down, acc, inbox, mail, sems, outs, mail_send, mail_recv, *scratch,
):
    total = two_all.shape[0]
    per = total // TILE
    one_scratch, two_scratch, ag = scratch[:11], scratch[11:22], scratch[22:34]
    ring = Ring()
    group, groups = ring.group, lax.axis_size("grp")
    line = Line(ring, *scratch[34:36])
    others = line.peers
    ring.barrier(others)

    one = Scatter(ring, mix_part, *one_scratch)
    second_sum = Scatter(ring, down_part, *two_scratch)
    u2, g2, u3, g3 = [
        Gather(ring, far_rows(far, ring, k, total), dst, *ag[3 * i : 3 * i + 3])
        for i, (far, k, dst) in enumerate(
            ((up_far, 2, up_two), (two_far, 2, two_two), (up_far, 3, up_three), (two_far, 3, two_three))
        )
    ]
    two_sources = (two_all, two_one, two_two, two_three)
    up_sources = (up_all, up_one, up_two, up_three)

    def first_norm():
        unit, scale = unit_of(tokens[...].astype(WIDE))
        incoming = one.total[...]
        tokens_grad[...] = (resid_back[...] + back_of(incoming, unit, scale, gains[0:1])).astype(LOW)
        four[...] = jnp.zeros_like(four)
        four[0:1] = jnp.sum(incoming * unit, axis=0, keepdims=True)
        four[1:2] = sums[0:1]
        four[2:3] = jnp.sum(incoming, axis=0, keepdims=True)
        four[3:4] = sums[1:2]

    def mail_copy(stage):
        peer = (ring.twin, ring.xn, ring.yn)[stage]
        return ring.copy(mail.at[stage], inbox.at[stage], mail_send, mail_recv, stage, peer)

    def mail_start(stage):
        mail[stage] = four[...]
        mail_copy(stage).start()

    def mail_wait(stage):
        mail_copy(stage).wait_recv()
        four[...] += inbox[stage]

    def group_copy(k):
        return pltpu.make_async_remote_copy(
            src_ref=mail.at[3],
            dst_ref=inbox.at[2 + k],
            send_sem=mail_send.at[2 + k],
            recv_sem=mail_recv.at[2 + k],
            device_id=others[k - 1],
            device_id_type=MESH_ID,
        )

    def group_start():
        four[4:5] = jnp.zeros((1, four.shape[1]), WIDE)
        local = bias_term.shape[1]
        for c in range(3):
            four[4:5, c * local : (c + 1) * local] = bias_term[c : c + 1, :]
        mail[3] = four[...]
        for k in range(1, groups):
            group_copy(k).start()

    def group_wait():
        for k in range(1, groups):
            group_copy(k).wait_recv()
        summed = jnp.zeros(four.shape, WIDE)
        for number in range(groups):
            term = mail[3]
            for k in range(1, groups):
                source = lax.rem(group + groups - k, groups)
                term = jnp.where(source == number, inbox[2 + k], term)
            summed = summed + term
        four[...] = summed
        for stage in range(3):
            mail_copy(stage).wait_send()
        for k in range(1, groups):
            group_copy(k).wait_send()

    share = out_sum.shape[0]

    def out_rows():
        return out_grad.at[pl.ds(pl.multiple_of(group * share, share), share), :]

    def out_keep():
        return pltpu.make_async_copy(out_sum, out_rows(), sems.at[2, 2])

    def out_start():
        for k in range(1, groups):
            line.copy(k, out_sum, out_rows()).start()
        out_keep().start()

    def layer_end():
        layer_out[...] = (resid[...] + second_sum.total[...]).astype(LOW)

    def stage(item, number):
        return lambda: item.stage(number)

    plan = {
        0: [out_start, stage(u2, 0)],
        3: [stage(u2, 1), stage(g2, 0)],
        4: [stage(u2, 2)],
        5: [stage(u2, 3)],
        6: [stage(g2, 1), stage(u3, 0)],
        7: [stage(g2, 2), stage(u2, 4)],
        8: [stage(g2, 3), stage(g2, 4), stage(u3, 1), stage(g3, 0)],
        9: [stage(u3, 2)],
        10: [stage(u3, 3), stage(one, 0)],
        11: [stage(g3, 1), stage(one, 1), stage(u3, 4)],
        12: [stage(g3, 2), stage(g3, 3), stage(g3, 4), stage(second_sum, 0)],
        13: [stage(one, 2), stage(second_sum, 1)],
        14: [stage(one, 3), first_norm, lambda: mail_start(0)],
        15: [lambda: mail_wait(0), lambda: mail_start(1), stage(second_sum, 2)],
    }

    def fetch(source, tile, side):
        start = tile * TILE if isinstance(tile, int) else pl.multiple_of(tile * TILE, TILE)
        rows = pl.ds(start, TILE)
        return [
            pltpu.make_async_copy(two_sources[source].at[rows, :], two.at[side], sems.at[side, 0]),
            pltpu.make_async_copy(up_sources[source].at[rows, :], up.at[side], sems.at[side, 1]),
        ]

    def fetch_kept(tile, side):
        start = tile * TILE if isinstance(tile, int) else pl.multiple_of(tile * TILE, TILE)
        return pltpu.make_async_copy(saved.at[:, :, pl.ds(start, TILE)], kept.at[side], sems.at[side, 2])

    weights = load([(wide_hbm, wide), (down_hbm, down)], sems.at[2])
    for copy in fetch(0, 0, 0) + [fetch_kept(0, 0)]:
        copy.start()
    acc[...] = jnp.zeros_like(acc)

    def add(side, trio):
        acc[2] += mm(trio[0], up[side])
        acc[0] += mm(trio[1], two[side])
        acc[1] += mm(trio[2], two[side])

    steps = per * groups

    def start_fetch(step):
        side = lax.rem(step, 2)
        for source in range(groups):

            @pl.when((step < steps) & (step // per == source))
            def _():
                for copy in fetch(source, lax.rem(step, per), side):
                    copy.start()
                if source == 0:
                    fetch_kept(lax.rem(step, per), side).start()

    def events(step):
        for at, acts in plan.items():

            @pl.when(step == at)
            def _():
                for act in acts:
                    act()


    def own_body(step, carry):
        events(step)
        side = lax.rem(step, 2)
        for copy in fetch(0, 0, side) + [fetch_kept(0, side)]:
            copy.wait()

        @pl.when(step + 1 < per)
        def _():
            start_fetch(step + 1)

        add(side, [kept[side, c] for c in range(3)])
        return carry

    lax.fori_loop(0, per, own_body, 0)
    for copy in weights:
        copy.wait()

    def body(step, carry):
        events(step)
        side = lax.rem(step, 2)

        @pl.when(lax.rem(step, per) == 0)
        def _():
            start_fetch(step)

        for copy in fetch(0, 0, side):
            copy.wait()

        @pl.when(lax.rem(step + 1, per) != 0)
        def _():
            start_fetch(step + 1)

        trio = forward_units(two[side], up[side], wide, down)
        add(side, trio)
        return carry

    lax.fori_loop(per, steps, body, 0)
    mail_wait(1)
    mail_start(2)
    wide[...] = acc[0:2].astype(LOW)
    copies = load([(wide, wide_grad)], outs)
    mail_wait(2)
    group_start()
    down[...] = acc[2].astype(LOW)
    copies += load([(down, down_grad)], outs.at[pl.ds(1, 1)])
    second_sum.stage(3)
    layer_end()
    group_wait()
    out_keep().wait()
    for k in range(1, groups):
        line.copy(k, out_sum, out_rows()).wait()
    for copy in copies:
        copy.wait()


def last(mix_part, down_part, tokens, resid, resid_back, gains, sums, bias_term, out_sum,
         two_all, up_all, saved, two_far, up_far, up_one, two_one, wide, down):
    total, width = two_all.shape
    rows = tokens.shape[0]
    local = down.shape[0]
    groups = lax.axis_size("grp")
    tall = (((total, width), LOW), ANY)
    block = (((rows, width), LOW), VM)
    return call(
        last_kernel,
        8,
        [(mix_part, ANY), (down_part, ANY)]
        + [(item, VM) for item in (tokens, resid, resid_back, gains, sums, bias_term, out_sum)]
        + [(item, ANY) for item in (two_all, up_all, saved, two_far, up_far, up_one, two_one, wide, down)],
        [
            block,
            block,
            (((8, width), WIDE), VM),
            (((out_sum.shape[0] * groups, width), LOW), ANY),
            (((2, local, width), LOW), ANY),
            (((local, width), LOW), ANY),
            tall, tall, tall, tall,
        ],
        [
            pltpu.VMEM((2, TILE, width), LOW),
            pltpu.VMEM((2, TILE, width), LOW),
            pltpu.VMEM((2, 3, local, TILE), LOW),
            pltpu.VMEM((2, local, width), LOW),
            pltpu.VMEM((local, width), LOW),
            pltpu.VMEM((3, local, width), WIDE),
            pltpu.VMEM((2 + groups, 8, width), WIDE),
            pltpu.VMEM((4, 8, width), WIDE),
            pltpu.SemaphoreType.DMA((3, 3)),
            pltpu.SemaphoreType.DMA((2,)),
            pltpu.SemaphoreType.DMA((2 + groups,)),
            pltpu.SemaphoreType.DMA((2 + groups,)),
        ]
        + scatter_scratch(rows, width) * 2
        + gather_sems() * N_LAST_GATHERS
        + line_sems(),
        limit=62,
        flops=72 << 30,
        cost=120 << 20,
    )


RING = 8


def on_device(
    tokens,
    norm_gains,
    norm_biases,
    mix_weight,
    mix_bias,
    out_weight,
    gate_up_weight,
    down_weight,
    row_lengths,
    row_group,
    cotangent,
):
    count = lax.axis_size("seq")
    shard = lax.axis_index("seq")
    group = lax.axis_index("grp")
    slots_dev = tokens.shape[0]
    load = jnp.sum(jnp.where(row_group == group, row_lengths, 0))
    slots = shard * slots_dev + jnp.arange(slots_dev, dtype=jnp.int32)
    upstream = jnp.where(slots[:, None] < load, cotangent, jnp.zeros_like(cotangent))
    mix_t = jnp.transpose(mix_weight, (1, 0, 2))
    wide_t = jnp.transpose(gate_up_weight, (1, 2, 0))

    up_far = lax.all_gather(upstream, "grp", axis=0, tiled=True)
    (
        query, key, value, attended, lse, normed_all, up_all, resid, two_all, two_mine,
        tables, lab_col, lab_row,
    ) = attend_heads(
        row_lengths, row_group, tokens, norm_gains, norm_biases, upstream, mix_t, out_weight, mix_bias, count
    )
    two_far = lax.all_gather(two_mine, "grp", axis=0, tiled=True)
    down_part, saved, up_one, resid_back, branch_all, sums = feed(
        two_all, up_all, wide_t, down_weight, up_far, resid, upstream, norm_gains
    )
    mixin, mix_term, out_sum, bias_term, two_one = attend_heads_back(
        branch_all, normed_all, out_weight, tables, lab_col, lab_row,
        (query, key, value, attended, lse), two_far,
    )
    mix_grad = lax.psum(mix_term, "grp")
    mix_part = jnp.einsum(
        "ctf,cdf->td", mixin, mix_t, preferred_element_type=jnp.float32
    ).astype(jnp.bfloat16)
    tokens_grad, layer_out, four, out_grad, wide_grad, down_grad = last(
        mix_part, down_part, tokens, resid, resid_back, norm_gains, sums, bias_term, out_sum,
        two_all, up_all, saved, two_far, up_far, up_one, two_one, wide_t, down_weight,
    )[:6]
    local = mix_bias.shape[1]
    return (
        layer_out,
        tokens_grad,
        four[0:2],
        four[2:4],
        jnp.transpose(mix_grad, (1, 0, 2)).astype(jnp.float32),
        four[4, : 3 * local].reshape(3, local),
        out_grad.astype(jnp.float32),
        jnp.transpose(wide_grad, (2, 0, 1)).astype(jnp.float32),
        down_grad.astype(jnp.float32),
    )


def solution(mesh):
    placed = (
        P(("grp", "seq"), None),
        P(),
        P(),
        P(None, None, "seq"),
        P(None, "seq"),
        P("seq", None),
        P(None, None, "seq"),
        P("seq", None),
        P(),
        P(),
        P(("grp", "seq"), None),
    )
    return jax.shard_map(
        on_device if mesh.shape["seq"] == RING else plain_device,
        mesh=mesh,
        in_specs=placed,
        out_specs=(
            P(("grp", "seq"), None),
            P(("grp", "seq"), None),
            P(),
            P(),
            P(None, None, "seq"),
            P(None, "seq"),
            P("seq", None),
            P(None, None, "seq"),
            P("seq", None),
        ),
        check_vma=False,
    )
```

profile of v0, /device:TPU:0, one launch (start us, length us, event | category | flops | bytes accessed | tf_op | source)
XLA Modules:
  0.0 366.3 jit_solution(12764417825345327901)
XLA Ops:
  7.2 0.0 all-gather.3.cloned.1.call-start
  7.2 1.3 fusion
  8.5 0.7 add_compare_fusion
  9.2 1.9 broadcast_select_fusion.upstream
  11.1 0.0 all-gather.3.cloned.1.call-update
  11.2 0.0 all-gather.5.cloned.1.call-start
  11.2 87.0 %shard_map.178 = (bf16[1024,256]{1,0:T(8,128)(2,1)}, bf16[1024,256]{1,0:T(8,128)(2,1)}, bf16[1024,256]{1,0:T(8,128)(2,1)}, bf16[1024,256]{1,0:T(8,128)(2,1)}, f3...) custom-call(s32[8]{0:T(128)} %row_lengths.1, ...), custom_call_target="tpu_custom_call" | custom-call | flops 7516192768 | bytes 20000000 | tf_op jit(solution)/shard_map/pallas_call | solution.py:667
  98.2 0.0 all-gather.5.cloned.1.call-update
  98.2 0.0 all-reduce.2.cloned.1.call-start
  98.2 0.0 all-gather.3.cloned.1.call-done.far.up_far
  98.3 69.3 %shard_map.179 = (bf16[1024,2048]{1,0:T(8,128)(2,1)}, bf16[3,704,1024]{2,1,0:T(8,128)(2,1)}, bf16[1024,2048]{1,0:T(8,128)(2,1)}, f32[128,2048]{1,0:T(8,128)}, bf...) custom-call(bf16[1024,2048]{1,0:T(8,128)(2,1)} %get-tuple-element.39.two_all, bf16[1024,2048]{1,0:T(8,128)(2,1)} %get-tuple-element.40.up_all, ...), custom_call_target="tpu_custom_call" | custom-call | flops 19327352832 | bytes 20000000 | tf_op jit(solution)/shard_map/pallas_call | solution.py:667
  167.6 0.0 all-gather.5.cloned.1.call-done.far.two_far
  167.6 0.0 copy-start.4
  167.7 32.6 %shard_map.180 = (bf16[3,1024,256]{2,1,0:T(8,128)(2,1)}, bf16[3,2048,256]{2,1,0:T(8,128)(2,1)}, bf16[64,2048]{1,0:T(8,128)(2,1)}, f32[3,256]{1,0:T(4,128)}, bf16[1024,2048]{1,0:T(8,128)(2,1)}) custom-call(bf16[1024,2048]{1,0:T(8,128)(2,1)} %get-tuple-element.42.branch_all, bf16[1024,2048]{1,0:T(8,128)(2,1)} %get-tuple-element.43.normed_all, ...), custom_call_target="tpu_custom_call" | custom-call | flops 17179869184 | bytes 20000000 | tf_op jit(solution)/shard_map/pallas_call | solution.py:667
  200.2 0.0 all-reduce.2.cloned.1.call-update
  200.3 0.0 copy-done.4
  200.3 6.4 %bitcast_convert_fusion.mix_part = bf16[1024,2048]{1,0:T(8,128)(2,1)} fusion(bf16[3,1024,256]{2,1,0:T(8,128)(2,1)} %get-tuple-element.53, bf16[2048,3,256]{2,0,1:T(8,128)(2,1)S(1)} %copy-done.4), kind=kOutput, calls=%fused_computation.1 | convolution fusion | flops 3223322624 | bytes 8912896 | tf_op jit(solution)/shard_map/ctf,cdf->td/dot_general | solution.py:1522
  206.7 127.6 %shard_map.181 = (bf16[128,2048]{1,0:T(8,128)(2,1)}, bf16[128,2048]{1,0:T(8,128)(2,1)}, f32[8,2048]{1,0:T(8,128)}, bf16[256,2048]{1,0:T(8,128)(2,1)}, bf16[2,704...) custom-call(bf16[1024,2048]{1,0:T(8,128)(2,1)} %bitcast_convert_fusi, ...), custom_call_target="tpu_custom_call" | custom-call | flops 77309411328 | bytes 125829120 | tf_op jit(solution)/shard_map/pallas_call | solution.py:667
  334.3 0.0 copy-start
  334.3 0.9 slice_reduce_fusion
  335.2 0.6 reshape_squeeze.3
  335.8 0.0 slice-start
  335.8 2.9 convert_element_type.24
  338.7 0.0 copy-done
  338.7 0.0 copy-start.3
  338.7 0.0 slice-start.1
  338.7 3.3 convert_element_type.27
  342.0 0.0 copy-done.3
  342.0 0.6 fusion.2
  342.7 0.0 slice-done
  342.7 0.0 slice-done.1
  342.7 6.0 %convert_bitcast_fusion = f32[2048,2,704]{0,2,1:T(8,128)} fusion(bf16[2,704,2048]{2,1,0:T(8,128)(2,1)S(1)} %bitcast.11), kind=kLoop, calls=%fused_computation | loop fusion | flops 2883584 | bytes 17301504 | tf_op jit(solution)/shard_map/convert_element_type | solution.py:1538
  348.7 0.0 copy-start.2
  348.7 0.0 copy-start.1
  348.7 4.2 %all-reduce.2.cloned.1.call-done = bf16[2048,3,256]{2,0,1:T(8,128)(2,1)} async-done(((bf16[2048,3,256]{2,0,1:T(8,128)(2,1)}), bf16[2048,3,256]{2,0,1:T(8,128)(2,1)}) %all-reduce.2.cloned.1.call-update) | async-done | bytes 3145744 | tf_op jit(solution)/shard_map/psum | solution.py:1521
  352.9 5.1 %convert_element_type.23 = f32[2048,3,256]{2,0,1:T(8,128)} convert(bf16[2048,3,256]{2,0,1:T(8,128)(2,1)} %all-reduce.2.cloned.1.call-done) | non-fusion elementwise | flops 1572864 | bytes 9437184 | tf_op jit(solution)/shard_map/convert_element_type | solution.py:1535
  358.0 0.0 copy-done.2
  358.0 0.8 copy.23
  358.8 0.0 copy-done.1
  358.8 0.8 copy.24
  (1 shorter events, 0.0 us)
Async XLA Ops:
  7.2 91.1 %all-gather.3.cloned.1.call-start = ((), (), s32[]{:S(2)}) async-start(), calls=%async_computation | async-start | bytes 2621440 | tf_op jit(solution)/shard_map/all_gather | solution.py:1506
  11.2 156.5 %all-gather.5.cloned.1.call-start = ((), (), s32[]{:S(2)}) async-start(), calls=%async_computation.1 | async-start | bytes 2621440 | tf_op jit(solution)/shard_map/all_gather | solution.py:1513
  98.2 254.7 %all-reduce.2.cloned.1.call-start = ((), (), s32[]{:S(2)}) async-start(), calls=%async_computation.2 | async-start | bytes 6291456 | tf_op jit(solution)/shard_map/psum | solution.py:1521
  167.6 32.6 %copy-start.4 = (bf16[2048,3,256]{2,0,1:T(8,128)(2,1)S(1)}, bf16[2048,3,256]{2,0,1:T(8,128)(2,1)}, u32[]{:S(2)}) copy-start(bf16[2048,3,256]{2,0,1:T(8,128)(2,1)} %param.14) | copy-start | bytes 9437188
  334.3 4.5 %copy-start = (bf16[704,2048]{1,0:T(8,128)(2,1)S(1)}, bf16[704,2048]{1,0:T(8,128)(2,1)}, u32[]{:S(2)}) copy-start(bf16[704,2048]{1,0:T(8,128)(2,1)} %get-tuple-element.68) | copy-start | bytes 8650756
  335.8 6.9 %slice-start = ((s8[5767168]{0:T(1024)(128)(4,1)}), s8[4194304]{0:T(1024)(128)(4,1)S(1)}, s32[]{:S(2)}) async-start(s8[5767168]{0:T(1024)(128)(4,1)} %bitcast.10), calls=%async_computation.3 | async-start | bytes 8388608
  338.7 3.3 copy-start.3
  338.7 3.9 %slice-start.1 = ((s8[5767168]{0:T(1024)(128)(4,1)}), s8[1572864]{0:T(1024)(128)(4,1)S(1)}, s32[]{:S(2)}) async-start(s8[5767168]{0:T(1024)(128)(4,1)} %bitcast.10), calls=%async_computation.4 | async-start | bytes 3145728
  348.7 9.3 %copy-start.2 = (bf16[128,2048]{1,0:T(8,128)(2,1)S(1)}, bf16[128,2048]{1,0:T(8,128)(2,1)}, u32[]{:S(2)}) copy-start(bf16[128,2048]{1,0:T(8,128)(2,1)} %get-tuple-element.80) | copy-start | bytes 1572868
  348.7 10.1 %copy-start.1 = (bf16[128,2048]{1,0:T(8,128)(2,1)S(1)}, bf16[128,2048]{1,0:T(8,128)(2,1)}, u32[]{:S(2)}) copy-start(bf16[128,2048]{1,0:T(8,128)(2,1)} %get-tuple-element.81) | copy-start | bytes 1572868
Sparse Core Ops, SparseCore 0:
  11.3 48.6 all-gather.2
  98.3 46.1 all-gather.4
  200.4 152.4 all-reduce.1
where the time goes:
time: 373 us; the launch traced here: 366 us
  Pallas kernels  316 us (85%)
  other arithmetic  21.3 us (6%)
  between operations  14 us (4%)
  matrix products  6.41 us (2%)
  waiting for transfers between devices  4.26 us (1%)
  local copies, waits for them, and re-layouts  3.74 us (1%)
    pallas_call x4, Pallas kernels, call(): pl.pallas_call(kernel, out_shape=tuple((jax.ShapeDtypeStruct(*shape) for...  316 us
  transfers between devices with their start and end apart: 3, of which 1 were waited for; matrix products, arithmetic and copies ran while one was open for 6% of the time, Pallas kernels for 77%

commit v1 on v0

--- a/solution.py
+++ b/solution.py
@@ -818,7 +818,7 @@
     lax.fori_loop(0, tiles, mix_body, 0)
     keep = pltpu.make_async_copy(normed, normed_all, sems.at[1])
     keep.start()
-    for i in range(tiles):
+    def tile(i):
         rows = pl.ds(i * TILE, TILE)
         span = (i + 1) * TILE
         q_at = i * TILE + lax.broadcasted_iota(jnp.int32, (TILE, span), 0)
@@ -848,13 +848,32 @@
         attended[rows, :] = low
         stats[rows, :] = logs
         stream.tiles[i] = mm(low, out_weight[...]).astype(LOW)
-        stream.ready(i)
-        if i >= 1:
-            upper.stage(i)
-    for which in range(3):
-        stream.go(which)
+
+    def attend_body(step, carry):
+        chip = chips[tiles - 1]
+        for i in range(tiles - 1):
+            chip = jnp.where(step == i, chips[i], chip)
+        for i in range(tiles):
+
+            @pl.when(chip == i)
+            def _():
+                tile(i)
+
+        stream.ready(chip)
+        for i in range(tiles):
+
+            @pl.when(step == i)
+            def _():
+                if i:
+                    stream.go(i - 1)
+                if i < 3:
+                    upper.stage(i + 1)
+
+        return carry
+
+    lax.fori_loop(0, tiles, attend_body, 0)
+    stream.cross()
     lse[...] = jnp.transpose(stats[...])[:8, :]
-    stream.cross()
     stream.finish()
     resid[...] = stream.total[...] + tokens[...].astype(WIDE)
     unit, _ = unit_of(resid[...])
@@ -1073,8 +1092,8 @@
 
 def feed_kernel(
     two_all, up_all, wide_hbm, down_hbm, far, resid, upstream, gains,
-    down_part, saved, far_one, resid_back, branch_all, sums,
-    two, up, wide, down, kept, stage, own, sems, outs, *scratch,
+    down_part, begun, far_one, resid_back, branch_all, sums,
+    two, up, wide, down, kept, acc, own, sems, outs, *scratch,
 ):
     total = two_all.shape[0]
     tiles = total // TILE
@@ -1089,9 +1108,10 @@
         return pl.ds(pl.multiple_of(chip * TILE, TILE), TILE)
 
     def tile_loads(step, chip):
+        rows = rows_of(chip)
         return [
-            pltpu.make_async_copy(two_all.at[rows_of(chip), :], two.at[step], sems.at[0, step]),
-            pltpu.make_async_copy(up_all.at[rows_of(chip), :], up.at[step], sems.at[1, step]),
+            pltpu.make_async_copy(two_all.at[rows, :], two.at[rows, :], sems.at[0, step]),
+            pltpu.make_async_copy(up_all.at[rows, :], up.at[rows, :], sems.at[1, step]),
         ]
 
     weights = load([(wide_hbm, wide), (down_hbm, down)], sems.at[2])
@@ -1113,7 +1133,7 @@
         chip = chip_at(step)
         for copy in tile_loads(step, chip):
             copy.wait()
-        trio = forward_units(two[step], up[step], wide, down)
+        trio = forward_units(two[rows_of(chip), :], up[rows_of(chip), :], wide, down)
         for c in range(3):
             kept[c, :, rows_of(chip)] = trio[c]
         for i in range(1, tiles):
@@ -1136,8 +1156,6 @@
         return carry
 
     lax.fori_loop(0, tiles, body, 0)
-    keep = pltpu.make_async_copy(kept, saved, outs.at[tiles])
-    keep.start()
     unit, scale = unit_of(resid[...])
     stream.finish()
     incoming = stream.total[...]
@@ -1148,17 +1166,36 @@
     sums[0:1] = jnp.sum(incoming * unit, axis=0, keepdims=True)
     sums[1:2] = jnp.sum(incoming, axis=0, keepdims=True)
 
+    stream.close()
+
+    def acc_body(i, carry):
+        columns = pl.ds(pl.multiple_of(i * TILE, TILE), TILE)
+        acc[0, :, columns] = mm(kept[1], two[:, columns])
+        acc[1, :, columns] = mm(kept[2], two[:, columns])
+        acc[2, :, columns] = mm(kept[0], up[:, columns])
+
+        @pl.when(i == pieces - 2)
+        def _():
+            branch.stage(1)
+
+        return carry
+
+    pieces = two.shape[1] // TILE
+    lax.fori_loop(0, pieces, acc_body, 0)
+    keep = pltpu.make_async_copy(acc, begun, outs.at[tiles])
+    keep.start()
+
     def down_copy(i):
         start = i * TILE if isinstance(i, int) else pl.multiple_of(i * TILE, TILE)
         rows = pl.ds(start, TILE)
-        return pltpu.make_async_copy(stage.at[i], down_part.at[rows, :], outs.at[i])
+        return pltpu.make_async_copy(stream.tiles.at[i], down_part.at[rows, :], outs.at[i])
 
     def down_body(i, carry):
-        stage[i] = mm(kept[0, :, rows_of(i)], down[...], TN).astype(LOW)
+        stream.tiles[i] = mm(kept[0, :, rows_of(i)], down[...], TN).astype(LOW)
         down_copy(i).start()
-        for number in (1, 2, 3):
-
-            @pl.when(i == number)
+        for number in (2, 3):
+
+            @pl.when(i == number - 1)
             def _():
                 branch.stage(number)
 
@@ -1167,7 +1204,6 @@
     lax.fori_loop(0, tiles, down_body, 0)
     branch.stage(4)
     gather.stage(4)
-    stream.close()
     keep.wait()
     for i in range(tiles):
         down_copy(i).wait()
@@ -1186,26 +1222,26 @@
         + [(item, VM) for item in (resid, upstream, gains)],
         [
             tall,
-            (((3, local, total), LOW), ANY),
+            (((3, local, width), WIDE), ANY),
             tall,
             (((rows, width), WIDE), VM),
             tall,
             (((2, width), WIDE), VM),
         ],
         [
-            pltpu.VMEM((tiles, TILE, width), LOW),
-            pltpu.VMEM((tiles, TILE, width), LOW),
+            pltpu.VMEM((total, width), LOW),
+            pltpu.VMEM((total, width), LOW),
             pltpu.VMEM((2, local, width), LOW),
             pltpu.VMEM((local, width), LOW),
             pltpu.VMEM((3, local, total), LOW),
-            pltpu.VMEM((tiles, TILE, width), LOW),
+            pltpu.VMEM((3, local, width), WIDE),
             pltpu.VMEM((rows, width), LOW),
             pltpu.SemaphoreType.DMA((3, tiles)),
             pltpu.SemaphoreType.DMA((1 + tiles,)),
         ]
         + stream_scratch(rows, width)
         + gather_sems() * 2,
-        limit=60,
+        limit=62,
         flops=18 << 30,
     )
 
@@ -1214,12 +1250,12 @@
 
 
 def last_kernel(
-    mix_part, down_part, tokens, resid, resid_back, gains, sums, bias_term, out_sum,
-    two_all, up_all, saved, two_far, up_far, up_one, two_one, wide_hbm, down_hbm,
-    tokens_grad, layer_out, four, out_grad, wide_grad, down_grad, two_two, two_three, up_two, up_three,
-    two, up, kept, wide, down, acc, inbox, mail, sems, outs, mail_send, mail_recv, *scratch,
+    mixin_hbm, mix_hbm, down_part, tokens, resid, resid_back, gains, sums, bias_term, out_sum,
+    begun, two_far, up_far, up_one, two_one, wide_hbm, down_hbm,
+    tokens_grad, layer_out, four, out_grad, wide_grad, down_grad, two_two, two_three, up_two, up_three, mix_part,
+    two, up, wide, down, acc, mixin, mix, shelf, inbox, mail, sems, outs, mail_send, mail_recv, *scratch,
 ):
-    total = two_all.shape[0]
+    total = two_one.shape[0]
     per = total // TILE
     one_scratch, two_scratch, ag = scratch[:11], scratch[11:22], scratch[22:34]
     ring = Ring()
@@ -1236,8 +1272,8 @@
             ((up_far, 2, up_two), (two_far, 2, two_two), (up_far, 3, up_three), (two_far, 3, two_three))
         )
     ]
-    two_sources = (two_all, two_one, two_two, two_three)
-    up_sources = (up_all, up_one, up_two, up_three)
+    two_sources = (two_one, two_two, two_three)
+    up_sources = (up_one, up_two, up_three)
 
     def first_norm():
         unit, scale = unit_of(tokens[...].astype(WIDE))
@@ -1298,38 +1334,90 @@
 
     share = out_sum.shape[0]
 
-    def out_rows():
-        return out_grad.at[pl.ds(pl.multiple_of(group * share, share), share), :]
+    def out_rows(number):
+        return out_grad.at[pl.ds(pl.multiple_of(number * share, share), share), :]
 
     def out_keep():
-        return pltpu.make_async_copy(out_sum, out_rows(), sems.at[2, 2])
-
-    def out_start():
-        for k in range(1, groups):
-            line.copy(k, out_sum, out_rows()).start()
-        out_keep().start()
+        return pltpu.make_async_copy(out_sum, out_rows(group), sems.at[2, 2])
+
+    def out_copy(phase, side):
+        number = group - phase * side
+        at = 0 if side > 0 else groups
+        return pltpu.make_async_remote_copy(
+            src_ref=out_sum if phase == 0 else out_rows(number),
+            dst_ref=out_rows(number),
+            send_sem=line.send.at[at + phase],
+            recv_sem=line.recv.at[at + phase],
+            device_id=(group + side, ring.me),
+            device_id_type=MESH_ID,
+        )
+
+    def goes(phase, side):
+        number, peer = group - phase * side, group + side
+        return (number >= 0) & (number < groups) & (peer >= 0) & (peer < groups)
+
+    def comes(phase, side):
+        number = group - (phase + 1) * side
+        return (number >= 0) & (number < groups)
+
+    def out_phase(phase):
+        for side in (1, -1):
+            if phase:
+
+                @pl.when(comes(phase - 1, side))
+                def _():
+                    out_copy(phase - 1, side).wait_recv()
+
+            if phase < groups - 1:
+
+                @pl.when(goes(phase, side))
+                def _():
+                    out_copy(phase, side).start()
+
+    def out_end():
+        out_keep().wait()
+        for phase in range(groups - 1):
+            for side in (1, -1):
+
+                @pl.when(goes(phase, side))
+                def _():
+                    out_copy(phase, side).wait_send()
 
     def layer_end():
         layer_out[...] = (resid[...] + second_sum.total[...]).astype(LOW)
 
+    def product():
+        for copy in mix_loads:
+            copy.wait()
+        copies = []
+        for i in range(per):
+            rows = pl.ds(i * TILE, TILE)
+            if i >= 2:
+                copies[i - 2].wait()
+            item = jnp.zeros((TILE, shelf.shape[2]), WIDE)
+            for c in range(3):
+                item = item + mm(mixin[c, rows, :], mix[c], NT)
+            shelf[i % 2] = item.astype(LOW)
+            copies.append(pltpu.make_async_copy(shelf.at[i % 2], mix_part.at[rows, :], sems.at[3, i % 2]))
+            copies[i].start()
+        for copy in copies[-2:]:
+            copy.wait()
+
     def stage(item, number):
         return lambda: item.stage(number)
 
     plan = {
-        0: [out_start, stage(u2, 0)],
-        3: [stage(u2, 1), stage(g2, 0)],
-        4: [stage(u2, 2)],
-        5: [stage(u2, 3)],
-        6: [stage(g2, 1), stage(u3, 0)],
-        7: [stage(g2, 2), stage(u2, 4)],
-        8: [stage(g2, 3), stage(g2, 4), stage(u3, 1), stage(g3, 0)],
-        9: [stage(u3, 2)],
-        10: [stage(u3, 3), stage(one, 0)],
-        11: [stage(g3, 1), stage(one, 1), stage(u3, 4)],
-        12: [stage(g3, 2), stage(g3, 3), stage(g3, 4), stage(second_sum, 0)],
-        13: [stage(one, 2), stage(second_sum, 1)],
-        14: [stage(one, 3), first_norm, lambda: mail_start(0)],
-        15: [lambda: mail_wait(0), lambda: mail_start(1), stage(second_sum, 2)],
+        1: [stage(u2, 1), stage(g2, 0)],
+        2: [stage(u2, 2), lambda: out_phase(1)],
+        3: [stage(u2, 3), stage(g2, 1)],
+        4: [stage(g2, 2), stage(u3, 0), stage(u2, 4), product, stage(g2, 3), stage(g2, 4), stage(g3, 0)],
+        5: [stage(u3, 1), lambda: out_phase(2)],
+        6: [stage(u3, 2), stage(g3, 1), stage(one, 0)],
+        7: [stage(u3, 3), stage(g3, 2), stage(one, 1)],
+        8: [stage(g3, 3), stage(u3, 4), stage(g3, 4), stage(second_sum, 0), lambda: out_phase(3)],
+        9: [stage(one, 2), stage(second_sum, 1)],
+        10: [stage(one, 3), first_norm, lambda: mail_start(0)],
+        11: [lambda: mail_wait(0), lambda: mail_start(1), stage(second_sum, 2)],
     }
 
     def fetch(source, tile, side):
@@ -1340,32 +1428,31 @@
             pltpu.make_async_copy(up_sources[source].at[rows, :], up.at[side], sems.at[side, 1]),
         ]
 
-    def fetch_kept(tile, side):
-        start = tile * TILE if isinstance(tile, int) else pl.multiple_of(tile * TILE, TILE)
-        return pltpu.make_async_copy(saved.at[:, :, pl.ds(start, TILE)], kept.at[side], sems.at[side, 2])
-
     weights = load([(wide_hbm, wide), (down_hbm, down)], sems.at[2])
-    for copy in fetch(0, 0, 0) + [fetch_kept(0, 0)]:
+    for copy in fetch(0, 0, 0):
         copy.start()
-    acc[...] = jnp.zeros_like(acc)
+    resume = pltpu.make_async_copy(begun, acc, outs.at[0])
+    resume.start()
+    mix_loads = load([(mixin_hbm, mixin), (mix_hbm, mix)], sems.at[4])
+    out_keep().start()
+    out_phase(0)
+    u2.stage(0)
 
     def add(side, trio):
         acc[2] += mm(trio[0], up[side])
         acc[0] += mm(trio[1], two[side])
         acc[1] += mm(trio[2], two[side])
 
-    steps = per * groups
+    steps = per * (groups - 1)
 
     def start_fetch(step):
         side = lax.rem(step, 2)
-        for source in range(groups):
+        for source in range(groups - 1):
 
             @pl.when((step < steps) & (step // per == source))
             def _():
                 for copy in fetch(source, lax.rem(step, per), side):
                     copy.start()
-                if source == 0:
-                    fetch_kept(lax.rem(step, per), side).start()
 
     def events(step):
         for at, acts in plan.items():
@@ -1376,28 +1463,15 @@
                     act()
 
 
-    def own_body(step, carry):
-        events(step)
-        side = lax.rem(step, 2)
-        for copy in fetch(0, 0, side) + [fetch_kept(0, side)]:
-            copy.wait()
-
-        @pl.when(step + 1 < per)
-        def _():
-            start_fetch(step + 1)
-
-        add(side, [kept[side, c] for c in range(3)])
-        return carry
-
-    lax.fori_loop(0, per, own_body, 0)
     for copy in weights:
         copy.wait()
+    resume.wait()
 
     def body(step, carry):
         events(step)
         side = lax.rem(step, 2)
 
-        @pl.when(lax.rem(step, per) == 0)
+        @pl.when((lax.rem(step, per) == 0) & (step > 0))
         def _():
             start_fetch(step)
 
@@ -1408,11 +1482,10 @@
         def _():
             start_fetch(step + 1)
 
-        trio = forward_units(two[side], up[side], wide, down)
-        add(side, trio)
+        add(side, forward_units(two[side], up[side], wide, down))
         return carry
 
-    lax.fori_loop(per, steps, body, 0)
+    lax.fori_loop(0, steps, body, 0)
     mail_wait(1)
     mail_start(2)
     wide[...] = acc[0:2].astype(LOW)
@@ -1424,16 +1497,14 @@
     second_sum.stage(3)
     layer_end()
     group_wait()
-    out_keep().wait()
-    for k in range(1, groups):
-        line.copy(k, out_sum, out_rows()).wait()
+    out_end()
     for copy in copies:
         copy.wait()
 
 
-def last(mix_part, down_part, tokens, resid, resid_back, gains, sums, bias_term, out_sum,
-         two_all, up_all, saved, two_far, up_far, up_one, two_one, wide, down):
-    total, width = two_all.shape
+def last(mixin, mix, down_part, tokens, resid, resid_back, gains, sums, bias_term, out_sum,
+         begun, two_far, up_far, up_one, two_one, wide, down):
+    total, width = two_one.shape
     rows = tokens.shape[0]
     local = down.shape[0]
     groups = lax.axis_size("grp")
@@ -1442,9 +1513,9 @@
     return call(
         last_kernel,
         8,
-        [(mix_part, ANY), (down_part, ANY)]
+        [(mixin, ANY), (mix, ANY), (down_part, ANY)]
         + [(item, VM) for item in (tokens, resid, resid_back, gains, sums, bias_term, out_sum)]
-        + [(item, ANY) for item in (two_all, up_all, saved, two_far, up_far, up_one, two_one, wide, down)],
+        + [(item, ANY) for item in (begun, two_far, up_far, up_one, two_one, wide, down)],
         [
             block,
             block,
@@ -1452,25 +1523,27 @@
             (((out_sum.shape[0] * groups, width), LOW), ANY),
             (((2, local, width), LOW), ANY),
             (((local, width), LOW), ANY),
-            tall, tall, tall, tall,
+            tall, tall, tall, tall, tall,
         ],
         [
             pltpu.VMEM((2, TILE, width), LOW),
             pltpu.VMEM((2, TILE, width), LOW),
-            pltpu.VMEM((2, 3, local, TILE), LOW),
             pltpu.VMEM((2, local, width), LOW),
             pltpu.VMEM((local, width), LOW),
             pltpu.VMEM((3, local, width), WIDE),
+            pltpu.VMEM(mixin.shape, LOW),
+            pltpu.VMEM(mix.shape, LOW),
+            pltpu.VMEM((2, TILE, width), LOW),
             pltpu.VMEM((2 + groups, 8, width), WIDE),
             pltpu.VMEM((4, 8, width), WIDE),
-            pltpu.SemaphoreType.DMA((3, 3)),
+            pltpu.SemaphoreType.DMA((5, 3)),
             pltpu.SemaphoreType.DMA((2,)),
             pltpu.SemaphoreType.DMA((2 + groups,)),
             pltpu.SemaphoreType.DMA((2 + groups,)),
         ]
         + scatter_scratch(rows, width) * 2
         + gather_sems() * N_LAST_GATHERS
-        + line_sems(),
+        + [pltpu.SemaphoreType.DMA((2 * groups,)), pltpu.SemaphoreType.DMA((2 * groups,))],
         limit=62,
         flops=72 << 30,
         cost=120 << 20,
@@ -1511,7 +1584,7 @@
         row_lengths, row_group, tokens, norm_gains, norm_biases, upstream, mix_t, out_weight, mix_bias, count
     )
     two_far = lax.all_gather(two_mine, "grp", axis=0, tiled=True)
-    down_part, saved, up_one, resid_back, branch_all, sums = feed(
+    down_part, begun, up_one, resid_back, branch_all, sums = feed(
         two_all, up_all, wide_t, down_weight, up_far, resid, upstream, norm_gains
     )
     mixin, mix_term, out_sum, bias_term, two_one = attend_heads_back(
@@ -1519,12 +1592,9 @@
         (query, key, value, attended, lse), two_far,
     )
     mix_grad = lax.psum(mix_term, "grp")
-    mix_part = jnp.einsum(
-        "ctf,cdf->td", mixin, mix_t, preferred_element_type=jnp.float32
-    ).astype(jnp.bfloat16)
     tokens_grad, layer_out, four, out_grad, wide_grad, down_grad = last(
-        mix_part, down_part, tokens, resid, resid_back, norm_gains, sums, bias_term, out_sum,
-        two_all, up_all, saved, two_far, up_far, up_one, two_one, wide_t, down_weight,
+        mixin, mix_t, down_part, tokens, resid, resid_back, norm_gains, sums, bias_term, out_sum,
+        begun, two_far, up_far, up_one, two_one, wide_t, down_weight,
     )[:6]
     local = mix_bias.shape[1]
     return (

time: 373 us -> 364 us (0.976)
  the two profiles are of different devices: /device:TPU:0 before, /device:TPU:26 now
where the time goes in v1:
time: 364 us; the launch traced here: 357 us
  Pallas kernels  317 us (87%)
  other arithmetic  21.4 us (6%)
  between operations  14.3 us (4%)
  local copies, waits for them, and re-layouts  3.73 us (1%)
    pallas_call x4, Pallas kernels, call(): pl.pallas_call(kernel, out_shape=tuple((jax.ShapeDtypeStruct(*shape) for...  317 us
  transfers between devices with their start and end apart: 3, of which 0 were waited for; matrix products, arithmetic and copies ran while one was open for 4% of the time, Pallas kernels for 79%

profile of v1, /device:TPU:26, one launch (start us, length us, event | category | flops | bytes accessed | tf_op | source)
XLA Modules:
  0.0 357.2 jit_solution(16369209962835925428)
XLA Ops:
  7.2 0.0 all-gather.3.cloned.1.call-start
  7.2 1.3 fusion
  8.5 0.7 add_compare_fusion
  9.2 1.9 broadcast_select_fusion.upstream
  11.1 0.0 all-gather.3.cloned.1.call-update
  11.2 0.0 all-gather.5.cloned.1.call-start
  11.2 80.0 %shard_map.178 = (bf16[1024,256]{1,0:T(8,128)(2,1)}, bf16[1024,256]{1,0:T(8,128)(2,1)}, bf16[1024,256]{1,0:T(8,128)(2,1)}, bf16[1024,256]{1,0:T(8,128)(2,1)}, f3...) custom-call(s32[8]{0:T(128)} %row_lengths.1, ...), custom_call_target="tpu_custom_call" | custom-call | flops 7516192768 | bytes 20000000 | tf_op jit(solution)/shard_map/pallas_call | solution.py:667
  91.2 0.0 all-gather.5.cloned.1.call-update
  91.2 0.2 all-reduce.2.cloned.1.call-start
  91.5 0.0 all-gather.3.cloned.1.call-done.far.up_far
  91.5 69.2 %shard_map.179 = (bf16[1024,2048]{1,0:T(8,128)(2,1)}, f32[3,704,2048]{2,1,0:T(8,128)}, bf16[1024,2048]{1,0:T(8,128)(2,1)}, f32[128,2048]{1,0:T(8,128)}, bf16[1024,2048]{1,0:T(8,128)(2,1)}, /*index=5*/f32[2,2048]{1,0:T(2,128)}) custom-call(bf16[1024,2048]{1,0:T(8,128)(2,1)} %get-tuple-element.39.two_all, bf16[1024,2048]{1,0:T(8,128)(2,1)} %get-tuple-element.40.up_all, ...), custom_call_target="tpu_custom_call" | custom-call | flops 19327352832 | bytes 20000000 | tf_op jit(solution)/shard_map/pallas_call | solution.py:667
  160.7 0.0 all-gather.5.cloned.1.call-done.far.two_far
  160.8 36.1 %shard_map.180 = (bf16[3,1024,256]{2,1,0:T(8,128)(2,1)}, bf16[3,2048,256]{2,1,0:T(8,128)(2,1)}, bf16[64,2048]{1,0:T(8,128)(2,1)}, f32[3,256]{1,0:T(4,128)}, bf16[1024,2048]{1,0:T(8,128)(2,1)}) custom-call(bf16[1024,2048]{1,0:T(8,128)(2,1)} %get-tuple-element.42.branch_all, bf16[1024,2048]{1,0:T(8,128)(2,1)} %get-tuple-element.43.normed_all, ...), custom_call_target="tpu_custom_call" | custom-call | flops 17179869184 | bytes 20000000 | tf_op jit(solution)/shard_map/pallas_call | solution.py:667
  196.9 0.0 all-reduce.2.cloned.1.call-update
  196.9 132.0 %shard_map.181 = (bf16[128,2048]{1,0:T(8,128)(2,1)}, bf16[128,2048]{1,0:T(8,128)(2,1)}, f32[8,2048]{1,0:T(8,128)}, bf16[256,2048]{1,0:T(8,128)(2,1)}, bf16[2,704...) custom-call(bf16[3,1024,256]{2,1,0:T(8,128)(2,1)} %get-tuple-element, ...), custom_call_target="tpu_custom_call" | custom-call | flops 77309411328 | bytes 125829120 | tf_op jit(solution)/shard_map/pallas_call | solution.py:667
  328.9 0.0 copy-start
  328.9 0.9 slice_reduce_fusion
  329.8 0.6 reshape_squeeze.3
  330.4 0.0 slice-start
  330.4 2.9 convert_element_type.20
  333.4 0.0 copy-done
  333.4 0.0 copy-start.3
  333.4 0.0 slice-start.1
  333.4 3.3 convert_element_type.23
  336.7 0.0 copy-done.3
  336.7 0.6 fusion.1
  337.3 0.0 slice-done
  337.3 0.0 slice-done.1
  337.3 6.0 %convert_bitcast_fusion = f32[2048,2,704]{0,2,1:T(8,128)} fusion(bf16[2,704,2048]{2,1,0:T(8,128)(2,1)S(1)} %bitcast.6), kind=kLoop, calls=%fused_computation | loop fusion | flops 2883584 | bytes 17301504 | tf_op jit(solution)/shard_map/convert_element_type | solution.py:1608
  343.3 0.0 copy-start.2
  343.3 0.0 copy-start.1
  343.3 0.0 all-reduce.2.cloned.1.call-done
  343.3 5.2 %convert_element_type.19 = f32[2048,3,256]{2,0,1:T(8,128)} convert(bf16[2048,3,256]{2,0,1:T(8,128)(2,1)} %all-reduce.2.cloned.1.call-done) | non-fusion elementwise | flops 1572864 | bytes 9437184 | tf_op jit(solution)/shard_map/convert_element_type | solution.py:1605
  348.5 0.0 copy-done.2
  348.6 0.8 copy.23
  349.3 0.0 copy-done.1
  349.3 0.8 copy.24
  (1 shorter events, 0.0 us)
Async XLA Ops:
  7.2 84.3 %all-gather.3.cloned.1.call-start = ((), (), s32[]{:S(2)}) async-start(), calls=%async_computation | async-start | bytes 2621440 | tf_op jit(solution)/shard_map/all_gather | solution.py:1579
  11.2 149.6 %all-gather.5.cloned.1.call-start = ((), (), s32[]{:S(2)}) async-start(), calls=%async_computation.1 | async-start | bytes 2621440 | tf_op jit(solution)/shard_map/all_gather | solution.py:1586
  91.2 252.1 %all-reduce.2.cloned.1.call-start = ((), (), s32[]{:S(2)}) async-start(), calls=%async_computation.2 | async-start | bytes 6291456 | tf_op jit(solution)/shard_map/psum | solution.py:1594
  328.9 4.5 %copy-start = (bf16[704,2048]{1,0:T(8,128)(2,1)S(1)}, bf16[704,2048]{1,0:T(8,128)(2,1)}, u32[]{:S(2)}) copy-start(bf16[704,2048]{1,0:T(8,128)(2,1)} %get-tuple-element.68) | copy-start | bytes 8650756
  330.4 6.9 %slice-start = ((s8[5767168]{0:T(1024)(128)(4,1)}), s8[4194304]{0:T(1024)(128)(4,1)S(1)}, s32[]{:S(2)}) async-start(s8[5767168]{0:T(1024)(128)(4,1)} %bitcast.5), calls=%async_computation.3 | async-start | bytes 8388608
  333.4 3.3 copy-start.3
  333.4 3.9 %slice-start.1 = ((s8[5767168]{0:T(1024)(128)(4,1)}), s8[1572864]{0:T(1024)(128)(4,1)S(1)}, s32[]{:S(2)}) async-start(s8[5767168]{0:T(1024)(128)(4,1)} %bitcast.5), calls=%async_computation.4 | async-start | bytes 3145728
  343.3 5.2 %copy-start.2 = (bf16[128,2048]{1,0:T(8,128)(2,1)S(1)}, bf16[128,2048]{1,0:T(8,128)(2,1)}, u32[]{:S(2)}) copy-start(bf16[128,2048]{1,0:T(8,128)(2,1)} %get-tuple-element.80) | copy-start | bytes 1572868
  343.3 6.0 %copy-start.1 = (bf16[128,2048]{1,0:T(8,128)(2,1)S(1)}, bf16[128,2048]{1,0:T(8,128)(2,1)}, u32[]{:S(2)}) copy-start(bf16[128,2048]{1,0:T(8,128)(2,1)} %get-tuple-element.81) | copy-start | bytes 1572868
Sparse Core Ops, SparseCore 0:
  11.3 44.7 all-gather.2
  91.4 43.7 all-gather.4
  197.0 135.9 all-reduce.1

commit v2 on v1

--- a/solution.py
+++ b/solution.py
@@ -1410,7 +1410,7 @@
         1: [stage(u2, 1), stage(g2, 0)],
         2: [stage(u2, 2), lambda: out_phase(1)],
         3: [stage(u2, 3), stage(g2, 1)],
-        4: [stage(g2, 2), stage(u3, 0), stage(u2, 4), product, stage(g2, 3), stage(g2, 4), stage(g3, 0)],
+        4: [stage(g2, 2), stage(u3, 0), stage(u2, 4), stage(g2, 3), stage(g2, 4), stage(g3, 0)],
         5: [stage(u3, 1), lambda: out_phase(2)],
         6: [stage(u3, 2), stage(g3, 1), stage(one, 0)],
         7: [stage(u3, 3), stage(g3, 2), stage(one, 1)],
@@ -1428,12 +1428,12 @@
             pltpu.make_async_copy(up_sources[source].at[rows, :], up.at[side], sems.at[side, 1]),
         ]
 
+    mix_loads = load([(mixin_hbm, mixin), (mix_hbm, mix)], sems.at[4])
     weights = load([(wide_hbm, wide), (down_hbm, down)], sems.at[2])
     for copy in fetch(0, 0, 0):
         copy.start()
     resume = pltpu.make_async_copy(begun, acc, outs.at[0])
     resume.start()
-    mix_loads = load([(mixin_hbm, mixin), (mix_hbm, mix)], sems.at[4])
     out_keep().start()
     out_phase(0)
     u2.stage(0)
@@ -1463,6 +1463,7 @@
                     act()
 
 
+    product()
     for copy in weights:
         copy.wait()
     resume.wait()
@@ -1553,6 +1554,44 @@
 RING = 8
 
 
+def mask_kernel(row_lengths, row_group, cotangent, upstream):
+    group = lax.axis_index("grp")
+    load = jnp.int32(0)
+    for row in range(row_lengths.shape[0]):
+        load = load + jnp.where(row_group[row] == group, row_lengths[row], 0)
+    first = lax.axis_index("seq") * cotangent.shape[0]
+    slots = first + lax.broadcasted_iota(jnp.int32, cotangent.shape, 0)
+    wide = cotangent[...].astype(jnp.float32)
+    upstream[...] = jnp.where(slots < load, wide, 0.0).astype(upstream.dtype)
+
+
+def mask_rows(row_lengths, row_group, cotangent):
+    return pl.pallas_call(
+        mask_kernel,
+        out_shape=jax.ShapeDtypeStruct(cotangent.shape, cotangent.dtype),
+        in_specs=[SM, SM, VM],
+        out_specs=VM,
+    )(row_lengths, row_group, cotangent)
+
+
+def widen_kernel(low, wide):
+    wide[...] = low[...].astype(jnp.float32)
+
+
+def widen(low, pieces):
+    rows, width = low.shape
+    spec = pl.BlockSpec((rows // pieces, width), lambda i: (i, 0))
+    return pl.pallas_call(
+        widen_kernel,
+        grid=(pieces,),
+        out_shape=jax.ShapeDtypeStruct(low.shape, jnp.float32),
+        in_specs=[spec],
+        out_specs=spec,
+        compiler_params=pltpu.CompilerParams(vmem_limit_bytes=32 << 20),
+        cost_estimate=pl.CostEstimate(flops=low.size, bytes_accessed=6 * low.size, transcendentals=0),
+    )(low)
+
+
 def on_device(
     tokens,
     norm_gains,
@@ -1567,12 +1606,7 @@
     cotangent,
 ):
     count = lax.axis_size("seq")
-    shard = lax.axis_index("seq")
-    group = lax.axis_index("grp")
-    slots_dev = tokens.shape[0]
-    load = jnp.sum(jnp.where(row_group == group, row_lengths, 0))
-    slots = shard * slots_dev + jnp.arange(slots_dev, dtype=jnp.int32)
-    upstream = jnp.where(slots[:, None] < load, cotangent, jnp.zeros_like(cotangent))
+    upstream = mask_rows(row_lengths, row_group, cotangent)
     mix_t = jnp.transpose(mix_weight, (1, 0, 2))
     wide_t = jnp.transpose(gate_up_weight, (1, 2, 0))
 
@@ -1602,11 +1636,11 @@
         tokens_grad,
         four[0:2],
         four[2:4],
-        jnp.transpose(mix_grad, (1, 0, 2)).astype(jnp.float32),
+        jnp.transpose(widen(mix_grad.reshape(-1, mix_grad.shape[2]), 6).reshape(mix_grad.shape), (1, 0, 2)),
         four[4, : 3 * local].reshape(3, local),
-        out_grad.astype(jnp.float32),
-        jnp.transpose(wide_grad, (2, 0, 1)).astype(jnp.float32),
-        down_grad.astype(jnp.float32),
+        widen(out_grad, 4),
+        jnp.transpose(widen(wide_grad.reshape(-1, wide_grad.shape[2]), 8).reshape(wide_grad.shape), (2, 0, 1)),
+        widen(down_grad, 4),
     )
 
 

time: 364 us -> 363 us (level)
  the two profiles are of different devices: /device:TPU:26 before, /device:TPU:10 now
where the time goes in v2:
time: 363 us; the launch traced here: 356 us
  Pallas kernels  334 us (92%)
  between operations  14.3 us (4%)
  local copies, waits for them, and re-layouts  7.13 us (2%)
    pallas_call x4, Pallas kernels, call(): pl.pallas_call(kernel, out_shape=tuple((jax.ShapeDtypeStruct(*shape) for...  319 us
    pallas_call x4, Pallas kernels, widen(): pl.pallas_call(widen_kernel, grid=(pieces,), out_shape=jax.ShapeDtypeStru...  13.4 us
  transfers between devices with their start and end apart: 3, of which 0 were waited for; matrix products, arithmetic and copies ran while one was open for 1% of the time, Pallas kernels for 82%

profile of v2, /device:TPU:10, one launch (start us, length us, event | category | flops | bytes accessed | tf_op | source)
XLA Modules:
  0.0 356.0 jit_solution(8092916289189982118)
XLA Ops:
  7.2 0.0 all-gather.3.cloned.1.call-start
  7.2 2.0 shard_map.178.upstream
  9.2 0.0 all-gather.3.cloned.1.call-update
  9.2 0.0 all-gather.5.cloned.1.call-start
  9.3 80.0 %shard_map.179 = (bf16[1024,256]{1,0:T(8,128)(2,1)}, bf16[1024,256]{1,0:T(8,128)(2,1)}, bf16[1024,256]{1,0:T(8,128)(2,1)}, bf16[1024,256]{1,0:T(8,128)(2,1)}, f3...) custom-call(s32[8]{0:T(128)} %row_lengths.3, ...), custom_call_target="tpu_custom_call" | custom-call | flops 7516192768 | bytes 20000000 | tf_op jit(solution)/shard_map/pallas_call | solution.py:667
  89.3 0.0 all-gather.5.cloned.1.call-update
  89.3 0.2 all-reduce.2.cloned.1.call-start
  89.5 0.0 all-gather.3.cloned.1.call-done.far.up_far
  89.6 69.3 %shard_map.180 = (bf16[1024,2048]{1,0:T(8,128)(2,1)}, f32[3,704,2048]{2,1,0:T(8,128)}, bf16[1024,2048]{1,0:T(8,128)(2,1)}, f32[128,2048]{1,0:T(8,128)}, bf16[1024,2048]{1,0:T(8,128)(2,1)}, /*index=5*/f32[2,2048]{1,0:T(2,128)}) custom-call(bf16[1024,2048]{1,0:T(8,128)(2,1)} %get-tuple-element.39.two_all, bf16[1024,2048]{1,0:T(8,128)(2,1)} %get-tuple-element.40.up_all, ...), custom_call_target="tpu_custom_call" | custom-call | flops 19327352832 | bytes 20000000 | tf_op jit(solution)/shard_map/pallas_call | solution.py:667
  158.8 0.0 all-gather.5.cloned.1.call-done.far.two_far
  158.9 36.2 %shard_map.181 = (bf16[3,1024,256]{2,1,0:T(8,128)(2,1)}, bf16[3,2048,256]{2,1,0:T(8,128)(2,1)}, bf16[64,2048]{1,0:T(8,128)(2,1)}, f32[3,256]{1,0:T(4,128)}, bf16[1024,2048]{1,0:T(8,128)(2,1)}) custom-call(bf16[1024,2048]{1,0:T(8,128)(2,1)} %get-tuple-element.42.branch_all, bf16[1024,2048]{1,0:T(8,128)(2,1)} %get-tuple-element.43.normed_all, ...), custom_call_target="tpu_custom_call" | custom-call | flops 17179869184 | bytes 20000000 | tf_op jit(solution)/shard_map/pallas_call | solution.py:667
  195.0 0.0 all-reduce.2.cloned.1.call-update
  195.1 133.4 %shard_map.182 = (bf16[128,2048]{1,0:T(8,128)(2,1)}, bf16[128,2048]{1,0:T(8,128)(2,1)}, f32[8,2048]{1,0:T(8,128)}, bf16[256,2048]{1,0:T(8,128)(2,1)}, bf16[2,704...) custom-call(bf16[3,1024,256]{2,1,0:T(8,128)(2,1)} %get-tuple-element, ...), custom_call_target="tpu_custom_call" | custom-call | flops 77309411328 | bytes 125829120 | tf_op jit(solution)/shard_map/pallas_call | solution.py:667
  328.5 0.0 copy-start.1
  328.5 0.9 slice_reduce_fusion
  329.4 0.6 reshape_squeeze.3
  330.0 0.0 copy-start.2
  330.0 1.2 copy-done.2
  331.2 0.0 slice-start
  331.2 1.8 shard_map.184
  333.1 0.0 copy-done.1
  333.1 0.0 slice-start.1
  333.1 2.9 shard_map.186
  335.9 0.0 slice-done
  335.9 0.3 slice-done.1
  336.2 0.0 copy-start.5
  336.2 5.2 %shard_map.185 = f32[1408,2048]{1,0:T(8,128)} custom-call(bf16[1408,2048]{1,0:T(8,128)(2,1)S(1)} %bitcast.12), custom_call_target="tpu_custom_call" | custom-call | flops 2883584 | bytes 17301504 | tf_op jit(solution)/shard_map/pallas_call | solution.py:1584
  341.5 0.0 copy-done.5
  341.5 0.6 fusion
  342.1 0.0 all-reduce.2.cloned.1.call-done.low
  342.1 0.0 copy-start
  342.1 1.9 copy-done
  344.0 0.0 copy-start.4
  344.0 0.0 copy-start.3
  344.0 3.5 shard_map.183
  347.5 0.0 copy-done.4
  347.5 0.8 copy.23
  348.3 0.0 copy-done.3
  348.3 0.8 copy.24
  (1 shorter events, 0.0 us)
Async XLA Ops:
  7.2 82.4 %all-gather.3.cloned.1.call-start = ((), (), s32[]{:S(2)}) async-start(), calls=%async_computation | async-start | bytes 2621440 | tf_op jit(solution)/shard_map/all_gather | solution.py:1613
  9.2 149.6 %all-gather.5.cloned.1.call-start = ((), (), s32[]{:S(2)}) async-start(), calls=%async_computation.1 | async-start | bytes 2621440 | tf_op jit(solution)/shard_map/all_gather | solution.py:1620
  89.3 252.8 %all-reduce.2.cloned.1.call-start = ((), (), s32[]{:S(2)}) async-start(), calls=%async_computation.2 | async-start | bytes 6291456 | tf_op jit(solution)/shard_map/psum | solution.py:1628
  328.5 4.6 %copy-start.1 = (bf16[704,2048]{1,0:T(8,128)(2,1)S(1)}, bf16[704,2048]{1,0:T(8,128)(2,1)}, u32[]{:S(2)}) copy-start(bf16[704,2048]{1,0:T(8,128)(2,1)} %get-tuple-element.68.low) | copy-start | bytes 8650756
  330.0 1.2 copy-start.2
  331.2 4.7 %slice-start = ((s8[5767168]{0:T(1024)(128)(4,1)}), s8[4194304]{0:T(1024)(128)(4,1)S(1)}, s32[]{:S(2)}) async-start(s8[5767168]{0:T(1024)(128)(4,1)} %bitcast.10), calls=%async_computation.3 | async-start | bytes 8388608
  333.1 3.2 slice-start.1
  336.2 5.2 %copy-start.5 = (f32[8,2048]{1,0:T(8,128)S(1)}, f32[8,2048]{1,0:T(8,128)}, u32[]{:S(2)}) copy-start(f32[8,2048]{1,0:T(8,128)} %get-tuple-element.64) | copy-start | bytes 196612
  342.1 1.9 copy-start
  344.0 3.5 copy-start.4
  344.0 4.3 %copy-start.3 = (bf16[128,2048]{1,0:T(8,128)(2,1)S(1)}, bf16[128,2048]{1,0:T(8,128)(2,1)}, u32[]{:S(2)}) copy-start(bf16[128,2048]{1,0:T(8,128)(2,1)} %get-tuple-element.81) | copy-start | bytes 1572868
Sparse Core Ops, SparseCore 0:
  10.2 45.4 all-gather.2
  89.4 44.5 all-gather.4
  195.2 133.6 all-reduce.1
